TPU v7x, 256 devices: a whole 4x4x8 slice. The times are simulated.
256 devices in a mesh: docs: 128 (over y, z_lo, x, core), pb: 2 (over z_hi).
Axes of the slice: x: 4, y: 4, z: 8 (z_hi: 2, z_lo: 4; z = z_hi * 4 + z_lo), core: 2. Of those that a mesh axis runs over, the one named last changes fastest.
Arguments:
- queries: bfloat16 [1024, 32, 128], P('docs', 'pb'), may hold values from -0.1875 to 0.1875
- documents: bfloat16 [16384, 64, 128], P('docs'), may hold values from -1.75 to 1.75
- lengths: int32 [16384], P('docs'), may hold values from 1 to 64
- pattern: int32 [8, 128], replicated, may hold values from 0 to 1
Outputs:
- scores: float32 [128, 8, 16384], P(None, 'pb', 'docs')
All inputs are finite; a program needn't handle non-finite values.
Results may differ from a plain program's by a relative error of at most 0.0003.
Values may be sent and summed in bfloat16 or wider, within the bound.
A program may use at most 64 MiB of HBM per device.

v0:
```python
import functools

import jax
import jax.numpy as jnp
from jax import lax
from jax.experimental import pallas as pl
from jax.experimental.pallas import tpu as pltpu
from jax.sharding import PartitionSpec as P

MESH = pl.DeviceIdType.MESH
CH = 64
NS = 8


def device(y, zl, x, c, h):
    return {"docs": ((y * 4 + zl) * 4 + x) * 2 + c, "pb": h}


def gather_kernel(q_ref, len_ref, d_hbm, q_out, dt_out, meta_out,
                  tmp, prep, docs, wide, dt, meta, meta_s, zs, zr, ss, sr, ts, tr, ls):
    idx = lax.axis_index("docs")
    zh = lax.axis_index("pb")
    c = idx % 2
    x = (idx // 2) % 4
    zl = (idx // 8) % 4
    y = idx // 32
    z = zh * 4 + zl
    xp, xm, yp, ym = (x + 1) % 4, (x + 3) % 4, (y + 1) % 4, (y + 3) % 4
    right, left = device(y, zl, xp, c, zh), device(y, zl, xm, c, zh)
    up, down = device(yp, zl, x, c, zh), device(ym, zl, x, c, zh)
    twin = device(y, zl, x, 1 - c, zh)
    column = []
    for s in range(1, 8):
        zt = (z + s) % 8
        column.append((zt // 4, device(y, zt % 4, x, c, zt // 4)))

    load = pltpu.make_async_copy(d_hbm, docs, ls.at[0])
    load.start()
    barrier = pltpu.get_barrier_semaphore()
    for d in [right, left, up, down, twin] + [d for _, d in column]:
        pl.semaphore_signal(barrier, inc=1, device_id=d, device_id_type=MESH)

    for h in range(2):
        for q in range(4):
            tmp[pl.ds(q, 16, stride=4), :] = q_ref[4 * h + q].astype(jnp.float32)
        prep[h] = tmp[...].astype(jnp.bfloat16)

    pl.semaphore_wait(barrier, 12)

    own = q_out.at[y, zl, x, zh]
    waits = []

    def send(src, dst, s_sem, r_sem, d):
        cp = pltpu.make_async_remote_copy(
            src_ref=src, dst_ref=dst, send_sem=s_sem, recv_sem=r_sem, device_id=d, device_id_type=MESH)
        cp.start()
        waits.append(cp)
        return cp

    first = [send(prep.at[ht], own, zs.at[s], zr.at[s], d) for s, (ht, d) in enumerate(column)]
    lc = pltpu.make_async_copy(prep.at[zh], own, ls.at[1])
    lc.start()

    lanes = jnp.broadcast_to(len_ref[...], (128, 128))
    cols = lanes.T
    r = lax.broadcasted_iota(jnp.int32, (128, 128), 0)
    k = lax.broadcasted_iota(jnp.int32, (128, 128), 1)
    ahead_col = (lanes > cols) | ((lanes == cols) & (k < r))
    ahead_row = (cols > lanes) | ((cols == lanes) & (r < k))
    rank_col = jnp.sum(jnp.where(ahead_col, 1, 0), axis=1, keepdims=True)
    rank_row = jnp.sum(jnp.where(ahead_row, 1, 0), axis=0, keepdims=True)
    here = rank_col == k
    meta[0:1] = jnp.sum(jnp.where(here, cols, 0), axis=0, keepdims=True)
    meta[1:2] = rank_row
    meta[2:3] = jnp.sum(jnp.where(here, r, 0), axis=0, keepdims=True)
    meta[3:8] = jnp.zeros((5, 128), jnp.int32)
    lm = pltpu.make_async_copy(meta, meta_s, ls.at[2])
    lm.start()
    lo = pltpu.make_async_copy(meta, meta_out.at[0], ls.at[3])
    lo.start()
    m0 = send(meta, meta_out.at[1], ts.at[0], tr.at[0], twin)
    lm.wait()
    load.wait()

    def arrange(g, _):
        for i in range(8):
            rows = docs[jnp.bitwise_and(meta_s[2, g * 8 + i], 127)].astype(jnp.float32)
            slot = lax.broadcasted_iota(jnp.int32, rows.shape, 0)
            wide[pl.ds(i, 64, stride=8), :] = jnp.where(slot < meta_s[0, g * 8 + i], rows, rows[0:1])
        for i in range(8):
            dt[g * 8 + i] = wide[i * CH:(i + 1) * CH].astype(jnp.bfloat16)
        return 0

    lax.fori_loop(0, 16, arrange, 0)
    ld = pltpu.make_async_copy(dt, dt_out.at[0], ls.at[4])
    ld.start()
    m1 = send(dt, dt_out.at[1], ts.at[1], tr.at[1], twin)

    lc.wait()
    for cp in first:
        cp.wait_recv()

    a = pl.ds(0, 2)
    b = pl.ds(2, 2)

    def pass_on(n, ref, d):
        return send(ref, ref, ss.at[n], sr.at[n], d)

    s0 = pass_on(0, q_out.at[y, a, x], right)
    s1 = pass_on(1, q_out.at[y, a, x], left)
    s2 = pass_on(2, q_out.at[y, b, x], up)
    s3 = pass_on(3, q_out.at[y, b, x], down)
    s0.wait_recv()
    s4 = pass_on(4, q_out.at[y, 0, xm], right)
    s1.wait_recv()
    s5 = pass_on(5, q_out.at[y, 1, xp], left)
    s2.wait_recv()
    s6 = pass_on(6, q_out.at[ym, 2, x], up)
    s3.wait_recv()
    s7 = pass_on(7, q_out.at[yp, 3, x], down)
    s4.wait_recv()
    s5.wait_recv()
    t0 = pass_on(8, q_out.at[y, a], up)
    t1 = pass_on(9, q_out.at[y, a], down)
    s6.wait_recv()
    s7.wait_recv()
    t2 = pass_on(10, q_out.at[:, b, x], right)
    t3 = pass_on(11, q_out.at[:, b, x], left)
    t0.wait_recv()
    t4 = pass_on(12, q_out.at[ym, 0], up)
    t1.wait_recv()
    t5 = pass_on(13, q_out.at[yp, 1], down)
    t2.wait_recv()
    t6 = pass_on(14, q_out.at[:, 2, xm], right)
    t3.wait_recv()
    t7 = pass_on(15, q_out.at[:, 3, xp], left)
    for cp in (m0, m1, t4, t5, t6, t7):
        cp.wait_recv()
    for cp in (lo, ld):
        cp.wait()
    for cp in waits:
        cp.wait_send()


def gather(queries, lengths, documents):
    hbm = pl.BlockSpec(memory_space=pl.ANY)
    vmem = pl.BlockSpec(memory_space=pltpu.VMEM)
    return pl.pallas_call(
        gather_kernel,
        name="gather_queries",
        out_shape=(
            jax.ShapeDtypeStruct((4, 4, 4, 2, 64, 128), jnp.bfloat16),
            jax.ShapeDtypeStruct((2, 128, CH, 128), jnp.bfloat16),
            jax.ShapeDtypeStruct((2, 8, 128), jnp.int32),
        ),
        in_specs=[vmem, vmem, hbm],
        out_specs=(hbm, hbm, hbm),
        scratch_shapes=[
            pltpu.VMEM((64, 128), jnp.float32),
            pltpu.VMEM((2, 64, 128), jnp.bfloat16),
            pltpu.VMEM((128, 64, 128), jnp.bfloat16),
            pltpu.VMEM((512, 128), jnp.float32),
            pltpu.VMEM((128, CH, 128), jnp.bfloat16),
            pltpu.VMEM((8, 128), jnp.int32),
            pltpu.SMEM((8, 128), jnp.int32),
            pltpu.SemaphoreType.DMA((7,)),
            pltpu.SemaphoreType.DMA((7,)),
            pltpu.SemaphoreType.DMA((16,)),
            pltpu.SemaphoreType.DMA((16,)),
            pltpu.SemaphoreType.DMA((2,)),
            pltpu.SemaphoreType.DMA((2,)),
            pltpu.SemaphoreType.DMA((5,)),
        ],
        compiler_params=pltpu.CompilerParams(collective_id=0, has_side_effects=True, vmem_limit_bytes=60 << 20),
    )(queries, lengths, documents)


def score_kernel(position, *refs):
    pl.run_scoped(
        functools.partial(score_body, position, *refs),
        *([pltpu.ACC(0)((CH, 256), jnp.float32)] * NS + [pltpu.ACC(1)((CH, 256), jnp.float32)] * NS),
    )


def score_body(position, pat_ref, meta_ref, q_hbm, dt_hbm, out_ref,
               qbuf, dt, amax, total, chunks, steps, pairs, sems, *accs):
    acc = (accs[:NS], accs[NS:])
    col = position()
    col = (col, col + 1 - 2 * (col % 2))

    def fetch(side):
        return pltpu.make_async_copy(dt_hbm.at[side], dt.at[pl.ds(side * 128, 128)], sems.at[8 + side])

    def rows_of(k):
        return pltpu.make_async_copy(q_hbm.at[k], qbuf.at[k], sems.at[k])

    def wanted(k):
        return (pat_ref[k, col[0]] > 0) | (pat_ref[k, col[1]] > 0)

    def start(k, _):
        @pl.when(wanted(k))
        def _():
            rows_of(k).start()

        return 0

    lax.fori_loop(0, 8, start, 0)
    fetch(0).start()
    fetch(1).start()
    count = jnp.int32(0)
    for side in range(2):
        def note(k, n, side=side):
            on = pat_ref[k, col[side]] > 0

            @pl.when(on)
            def _():
                pairs[n] = side * 8 + k

            return n + on.astype(jnp.int32)

        count = lax.fori_loop(0, 8, note, count)

        def list_group(g, t, side=side):
            need = (meta_ref[side, 0, g * 8] + 7) // 8

            def put(i, t):
                chunks[side, t] = side * 128 + g * 8 + i
                return t + 1

            return lax.fori_loop(0, need, put, t)

        t = lax.fori_loop(0, 16, list_group, 0)
        for i in range(NS):
            chunks[side, t + i] = chunks[side, t - 1]
        steps[side] = (t + NS - 1) // NS
    units = count * 2
    out_ref[...] = jnp.zeros_like(out_ref)
    total[...] = jnp.zeros_like(total)
    amax[...] = jnp.full_like(amax, -jnp.inf)

    def arrive(k, _):
        @pl.when(wanted(k))
        def _():
            rows_of(k).wait()

        return 0

    lax.fori_loop(0, 8, arrive, 0)
    fetch(0).wait()
    fetch(1).wait()

    def weights(u):
        k = pairs[u // 2] % 8
        for m in range(2):
            j = pl.multiple_of(((u % 2) * 2 + m) * 32, 32)
            w = qbuf[k, :, pl.ds(j, 32), :].reshape(256, 128)
            pltpu.matmul_push_rhs(jnp.concatenate([w, jnp.zeros_like(w)], axis=1), 0, m, transpose=True)

    def push(side, step, s, head=False):
        w = dt[chunks[side, step * NS + s]]
        w = jnp.concatenate([w, jnp.zeros_like(w)], axis=1)
        for m in range(2):
            if head:
                pltpu.matmul_acc_lhs(acc[m][s], w, load_staged_rhs=0)
            else:
                pltpu.matmul_acc_lhs(acc[m][s], w)

    def pop(side, step, s):
        g = (chunks[side, step * NS + s] // 8) % 16
        for m in range(2):
            r = pltpu.matmul_pop(acc[m][s])
            r = jnp.max(r.reshape(8, 8, 256), axis=0)
            amax[g, m] = jnp.maximum(amax[g, m], r)

    def close(slot):
        total[slot] += amax[:, 0] + amax[:, 1]
        amax[...] = jnp.full_like(amax, -jnp.inf)

    @pl.when(count > 0)
    def _():
        weights(0)

        def unit(u, state):
            side0, last0, slot0 = state
            slot = pairs[u // 2]
            side = slot // 8
            for s in range(NS):
                pop(side0, last0, s)
                push(side, 0, s, head=s == 0)
            weights(jnp.minimum(u + 1, units - 1))
            close(slot0)

            def half(m, _):
                for s in range(NS):
                    pop(side, m - 1, s)
                    push(side, m, s)
                return 0

            lax.fori_loop(1, steps[side], half, 0)
            return side, steps[side] - 1, slot

        zero = jnp.int32(0)
        side, last, slot = lax.fori_loop(0, units, unit, (zero, zero, zero + 16))
        for s in range(NS):
            pop(side, last, s)
        close(slot)
        push(0, 0, 0, head=True)
        pltpu.matmul_pop(acc[0][0])
        pltpu.matmul_pop(acc[1][0])

        def finish(i, _):
            slot = pairs[i]
            sums = total[slot].reshape(128, 256)
            for part in range(2):
                turned = sums[:, part * 128:(part + 1) * 128].T.reshape(4, 4, 8, 128)
                folded = (turned[:, 0] + turned[:, 1]) + (turned[:, 2] + turned[:, 3])
                folded = folded[:, 0:4] + folded[:, 4:8]
                out_ref[slot, pl.ds(part * 16, 16)] = folded.reshape(16, 128)
            return 0

        lax.fori_loop(0, count, finish, 0)


def score(position, pattern, meta, rows, dt):
    smem = pl.BlockSpec(memory_space=pltpu.SMEM)
    hbm = pl.BlockSpec(memory_space=pl.ANY)
    return pl.pallas_call(
        functools.partial(score_kernel, position),
        name="score_blocks",
        out_shape=jax.ShapeDtypeStruct((16, 32, 128), jnp.float32),
        in_specs=[smem, smem, hbm, hbm],
        out_specs=pl.BlockSpec(memory_space=pltpu.VMEM),
        scratch_shapes=[
            pltpu.VMEM((8, 8, 128, 128), jnp.bfloat16),
            pltpu.VMEM((256, CH, 128), jnp.bfloat16),
            pltpu.VMEM((16, 2, 8, 256), jnp.float32),
            pltpu.VMEM((17, 16, 8, 256), jnp.float32),
            pltpu.SMEM((2, 128 + NS), jnp.int32),
            pltpu.SMEM((2,), jnp.int32),
            pltpu.SMEM((16,), jnp.int32),
            pltpu.SemaphoreType.DMA((10,)),
        ],
        compiler_params=pltpu.CompilerParams(vmem_limit_bytes=60 << 20),
    )(pattern, meta, rows, dt)


def swap_kernel(part_ref, meta_ref, out_ref, got, s_sem, r_sem):
    idx = lax.axis_index("docs")
    c = idx % 2
    twin = {"docs": idx + 1 - 2 * c, "pb": lax.axis_index("pb")}
    barrier = pltpu.get_barrier_semaphore()
    pl.semaphore_signal(barrier, inc=1, device_id=twin, device_id_type=MESH)
    pl.semaphore_wait(barrier, 1)
    cp = pltpu.make_async_remote_copy(
        src_ref=part_ref.at[pl.ds(8, 8)], dst_ref=got, send_sem=s_sem, recv_sem=r_sem,
        device_id=twin, device_id_type=MESH)
    cp.start()
    rank = jnp.broadcast_to(meta_ref[0, 1:2], (32, 128))

    def place(value, k, core):
        back = jnp.take_along_axis(value, rank, axis=1).reshape(8, 4, 128)
        for h in range(8):
            out_ref[k * 16 + h * 2 + core] = back[h]

    for k in range(8):
        place(part_ref[k], k, c)
    cp.wait_recv()
    for k in range(8):
        place(got[k], k, 1 - c)
    cp.wait_send()


def swap(part, meta):
    vmem = pl.BlockSpec(memory_space=pltpu.VMEM)
    return pl.pallas_call(
        swap_kernel,
        name="swap_scores",
        out_shape=jax.ShapeDtypeStruct((128, 4, 128), jnp.float32),
        in_specs=[vmem, vmem],
        out_specs=vmem,
        scratch_shapes=[
            pltpu.VMEM((8, 32, 128), jnp.float32),
            pltpu.SemaphoreType.DMA,
            pltpu.SemaphoreType.DMA,
        ],
        compiler_params=pltpu.CompilerParams(collective_id=1, has_side_effects=True),
    )(part, meta)


def local(queries, documents, lengths, pattern):
    rows, dt, meta = gather(queries, lengths.reshape(1, 128), documents)
    part = score(lambda: lax.axis_index("docs"), pattern, meta, rows.reshape(8, 8, 128, 128), dt)
    return swap(part, meta)


def solution(mesh):
    return jax.shard_map(
        local,
        mesh=mesh,
        in_specs=(P("docs", "pb", None), P("docs", None, None), P("docs"), P()),
        out_specs=P(None, "pb", "docs"),
        check_vma=False,
    )
```

profile of v0, /device:TPU:117, one launch (start us, length us, event | category | flops | bytes accessed | tf_op | source)
XLA Modules:
  0.0 66.6 jit_solution(4260455752535605967)
XLA Ops:
  0.0 26.7 %gather_queries.1 = (bf16[4,4,4,2,64,128]{5,4,3,2,1,0:T(8,128)(2,1)}, bf16[2,128,64,128]{3,2,1,0:T(8,128)(2,1)}, s32[2,8,128]{2,1,0:T(8,128)}) custom-call(bf16[8,16,128]{2,1,0:T(8,128)(2,1)} %q_ref.1, s32[1,128]{1,0:T(1,128)} %bitcast.3, bf16[128,64,128]{2,1,0:T(8,128)(2,1)} %d_hbm.1), custom_call_target="tpu_custom_call" | custom-call | tf_op jit(solution)/shard_map/gather_queries/pallas_call | solution.py:148
  26.7 30.2 %score_blocks.1.part_ref = f32[16,32,128]{2,1,0:T(8,128)} custom-call(s32[8,128]{1,0:T(8,128)} %refs_0_.1, s32[2,8,128]{2,1,0:T(8,128)} %get-tuple-element.8.refs_1_.meta_ref, bf16[8,8,128,128]{3,2,1,0:T(8,128)(2,1)} %bitcast.2, bf16[2,128,64,128]{3,2,1,0:T(8,128)(2,1)} %get-tuple-element.10.refs_3_), custom_call_target="tpu_custom_call" | custom-call | tf_op jit(solution)/shard_map/score_blocks/pallas_call | solution.py:327
  56.9 8.0 %swap_scores.1 = f32[128,4,128]{2,1,0:T(4,128)} custom-call(f32[16,32,128]{2,1,0:T(8,128)} %score_blocks.1.part_ref, s32[2,8,128]{2,1,0:T(8,128)} %get-tuple-element.8.refs_1_.meta_ref), custom_call_target="tpu_custom_call" | custom-call | tf_op jit(solution)/shard_map/swap_scores/pallas_call | solution.py:375
  65.0 1.7 %copy.6 = f32[128,4,128]{2,1,0:T(4,128)} copy(f32[128,4,128]{2,1,0:T(4,128)} %swap_scores.1) | data formatting | bytes 524288
where the time goes:
time: 66.9 us; the launch traced here: 66.6 us
  Pallas kernels  65 us (97%)
  local copies, waits for them, and re-layouts  1.67 us (2%)
    pallas_call x1, Pallas kernels, score(): pl.pallas_call(functools.partial(score_kernel, position), name='score_blo...  30.2 us
    pallas_call x1, Pallas kernels, gather(): pl.pallas_call(gather_kernel, name='gather_queries', out_shape=(jax.Shape...  26.7 us
    pallas_call x1, Pallas kernels, swap(): pl.pallas_call(swap_kernel, name='swap_scores', out_shape=jax.ShapeDtypeS...  8.05 us
    unnamed x1, local copies, waits for them, and re-layouts  1.67 us

commit v1 on v0

v1 whole, which is shorter than its diff:
```python
import functools

import jax
import jax.numpy as jnp
from jax import lax
from jax.experimental import pallas as pl
from jax.experimental.pallas import tpu as pltpu
from jax.sharding import PartitionSpec as P

MESH = pl.DeviceIdType.MESH
CH = 64
NS = 8


def device(y, zl, x, c, h):
    return {"docs": ((y * 4 + zl) * 4 + x) * 2 + c, "pb": h}


def gather_kernel(q_hbm, len_hbm, d_hbm, q_out, dt_out, meta_out,
                  q_ref, len_ref, tmp, prep, docs, wide, dt, meta, meta_s, zs, zr, ss, sr, ts, tr, ls):
    loads = [pltpu.make_async_copy(src, dst, ls.at[5 + n])
             for n, (src, dst) in enumerate(((q_hbm, q_ref), (len_hbm, len_ref), (d_hbm, docs)))]
    for cp in loads:
        cp.start()
    idx = lax.axis_index("docs")
    zh = lax.axis_index("pb")
    c = idx % 2
    x = (idx // 2) % 4
    zl = (idx // 8) % 4
    y = idx // 32
    z = zh * 4 + zl
    xp, xm, yp, ym = (x + 1) % 4, (x + 3) % 4, (y + 1) % 4, (y + 3) % 4
    x2, y2 = (x + 2) % 4, (y + 2) % 4
    right, left = device(y, zl, xp, c, zh), device(y, zl, xm, c, zh)
    up, down = device(yp, zl, x, c, zh), device(ym, zl, x, c, zh)
    twin = device(y, zl, x, 1 - c, zh)
    column = []
    for s in (4, 3, 5, 2, 6, 1, 7):
        zt = (z + s) % 8
        column.append((zt // 4, device(y, zt % 4, x, c, zt // 4)))

    barrier = pltpu.get_barrier_semaphore()
    for d in [d for _, d in column] + [right, left, up, down, twin]:
        pl.semaphore_signal(barrier, inc=1, device_id=d, device_id_type=MESH)

    loads[0].wait()
    for h in range(2):
        for q in range(4):
            tmp[pl.ds(q, 16, stride=4), :] = q_ref[4 * h + q].astype(jnp.float32)
        prep[h] = tmp[...].astype(jnp.bfloat16)

    pl.semaphore_wait(barrier, 12)

    own = q_out.at[y, zl, x, zh]
    waits = []

    def send(src, dst, s_sem, r_sem, d):
        cp = pltpu.make_async_remote_copy(
            src_ref=src, dst_ref=dst, send_sem=s_sem, recv_sem=r_sem, device_id=d, device_id_type=MESH)
        cp.start()
        waits.append(cp)
        return cp

    first = [send(prep.at[ht], own, zs.at[s], zr.at[s], d) for s, (ht, d) in enumerate(column)]
    lc = pltpu.make_async_copy(prep.at[zh], own, ls.at[1])
    lc.start()

    loads[1].wait()
    lanes = jnp.broadcast_to(len_ref[...], (128, 128))
    cols = lanes.T
    r = lax.broadcasted_iota(jnp.int32, (128, 128), 0)
    k = lax.broadcasted_iota(jnp.int32, (128, 128), 1)
    ahead_col = (lanes > cols) | ((lanes == cols) & (k < r))
    ahead_row = (cols > lanes) | ((cols == lanes) & (r < k))
    rank_col = jnp.sum(jnp.where(ahead_col, 1, 0), axis=1, keepdims=True)
    rank_row = jnp.sum(jnp.where(ahead_row, 1, 0), axis=0, keepdims=True)
    here = rank_col == k
    sizes = jnp.sum(jnp.where(here, cols, 0), axis=0, keepdims=True)
    spread = jnp.broadcast_to(sizes, (128, 128))
    need = jnp.where(k % 8 == 0, (spread + 7) // 8, 0)
    steps = jnp.sum(need, axis=1, keepdims=True)[0:1]
    ends = jnp.sum(jnp.where(k <= r, need, 0), axis=1, keepdims=True)
    skip = jnp.where(r % 8 == 0, 8 - (spread.T + 7) // 8, 0)
    place = jnp.minimum(k, steps - 1)
    listed = place[0:1] + jnp.sum(jnp.where(ends <= place, skip, 0), axis=0, keepdims=True)
    meta[0:1] = sizes
    meta[1:2] = rank_row
    meta[2:3] = jnp.sum(jnp.where(here, r, 0), axis=0, keepdims=True)
    meta[3:4] = listed
    meta[4:5] = jnp.broadcast_to(steps, (1, 128))
    meta[5:8] = jnp.zeros((3, 128), jnp.int32)
    lm = pltpu.make_async_copy(meta, meta_s, ls.at[2])
    lm.start()
    lo = pltpu.make_async_copy(meta, meta_out.at[0], ls.at[3])
    lo.start()
    m0 = send(meta, meta_out.at[1], ts.at[0], tr.at[0], twin)
    lm.wait()
    loads[2].wait()

    def arrange(g, _):
        for i in range(8):
            rows = docs[jnp.bitwise_and(meta_s[2, g * 8 + i], 127)].astype(jnp.float32)
            slot = lax.broadcasted_iota(jnp.int32, rows.shape, 0)
            wide[pl.ds(i, 64, stride=8), :] = jnp.where(slot < meta_s[0, g * 8 + i], rows, rows[0:1])
        for i in range(8):
            dt[g * 8 + i] = wide[i * CH:(i + 1) * CH].astype(jnp.bfloat16)
        return 0

    lax.fori_loop(0, 16, arrange, 0)
    ld = pltpu.make_async_copy(dt, dt_out.at[0], ls.at[4])
    ld.start()
    m1 = send(dt, dt_out.at[1], ts.at[1], tr.at[1], twin)

    lc.wait()
    for cp in first:
        cp.wait_recv()

    a = pl.ds(0, 2)
    b = pl.ds(2, 2)
    used = [0]

    def pass_on(ref, d):
        n = used[0]
        used[0] += 1
        return send(ref, ref, ss.at[n], sr.at[n], d)

    def spread_a(xs):
        return pass_on(q_out.at[y, a, xs], up), pass_on(q_out.at[y, a, xs], down)

    def spread_b(ys):
        return pass_on(q_out.at[ys, b, x], right), pass_on(q_out.at[ys, b, x], left)

    def relay_a(xs, pair):
        pair[0].wait_recv()
        f = pass_on(q_out.at[ym, 0, xs], up)
        pair[1].wait_recv()
        return f, pass_on(q_out.at[yp, 1, xs], down)

    def relay_b(ys, pair):
        pair[0].wait_recv()
        f = pass_on(q_out.at[ys, 2, xm], right)
        pair[1].wait_recv()
        return f, pass_on(q_out.at[ys, 3, xp], left)

    s0 = pass_on(q_out.at[y, a, x], right)
    s1 = pass_on(q_out.at[y, a, x], left)
    s2 = pass_on(q_out.at[y, b, x], up)
    s3 = pass_on(q_out.at[y, b, x], down)
    a0 = spread_a(x)
    b0 = spread_b(y)
    s0.wait_recv()
    s4 = pass_on(q_out.at[y, 0, xm], right)
    s1.wait_recv()
    s5 = pass_on(q_out.at[y, 1, xp], left)
    s2.wait_recv()
    s6 = pass_on(q_out.at[ym, 2, x], up)
    s3.wait_recv()
    s7 = pass_on(q_out.at[yp, 3, x], down)
    a1 = spread_a(xm)
    a2 = spread_a(xp)
    b1 = spread_b(ym)
    b2 = spread_b(yp)
    s4.wait_recv()
    s5.wait_recv()
    a3 = spread_a(x2)
    s6.wait_recv()
    s7.wait_recv()
    b3 = spread_b(y2)
    last = []
    for xs, ys, pa, pb in ((x, y, a0, b0), (xm, ym, a1, b1), (xp, yp, a2, b2), (x2, y2, a3, b3)):
        last.extend(relay_a(xs, pa))
        last.extend(relay_b(ys, pb))
    for cp in [m0, m1] + last:
        cp.wait_recv()
    for cp in (lo, ld):
        cp.wait()
    for cp in waits:
        cp.wait_send()


def gather(queries, lengths, documents):
    hbm = pl.BlockSpec(memory_space=pltpu.HBM)
    free = pl.BlockSpec(memory_space=pl.ANY)
    return pl.pallas_call(
        gather_kernel,
        name="gather_queries",
        out_shape=(
            jax.ShapeDtypeStruct((4, 4, 4, 2, 64, 128), jnp.bfloat16),
            jax.ShapeDtypeStruct((2, 128, CH, 128), jnp.bfloat16),
            jax.ShapeDtypeStruct((2, 8, 128), jnp.int32),
        ),
        in_specs=[hbm, hbm, hbm],
        out_specs=(free, free, free),
        scratch_shapes=[
            pltpu.VMEM((8, 16, 128), jnp.bfloat16),
            pltpu.VMEM((1, 128), jnp.int32),
            pltpu.VMEM((64, 128), jnp.float32),
            pltpu.VMEM((2, 64, 128), jnp.bfloat16),
            pltpu.VMEM((128, 64, 128), jnp.bfloat16),
            pltpu.VMEM((512, 128), jnp.float32),
            pltpu.VMEM((128, CH, 128), jnp.bfloat16),
            pltpu.VMEM((8, 128), jnp.int32),
            pltpu.SMEM((8, 128), jnp.int32),
            pltpu.SemaphoreType.DMA((7,)),
            pltpu.SemaphoreType.DMA((7,)),
            pltpu.SemaphoreType.DMA((40,)),
            pltpu.SemaphoreType.DMA((40,)),
            pltpu.SemaphoreType.DMA((2,)),
            pltpu.SemaphoreType.DMA((2,)),
            pltpu.SemaphoreType.DMA((8,)),
        ],
        compiler_params=pltpu.CompilerParams(collective_id=0, has_side_effects=True, vmem_limit_bytes=12 << 20),
    )(*[pltpu.with_memory_space_constraint(v, pltpu.HBM) for v in (queries, lengths, documents)])


def score_kernel(position, *refs):
    pl.run_scoped(
        functools.partial(score_body, position, *refs),
        *([pltpu.ACC(0)((CH, 256), jnp.float32)] * NS + [pltpu.ACC(1)((CH, 256), jnp.float32)] * NS),
    )


def score_body(position, pat_ref, meta_ref, rows, dt, out_ref, amax, total, pairs, *accs):
    acc = (accs[:NS], accs[NS:])
    col = position()
    col = (col, col + 1 - 2 * (col % 2))

    count = jnp.int32(0)
    for side in range(2):
        def note(k, n, side=side):
            on = pat_ref[k, col[side]] > 0

            @pl.when(on)
            def _():
                pairs[n] = side * 8 + k

            return n + on.astype(jnp.int32)

        count = lax.fori_loop(0, 8, note, count)
    steps = [(meta_ref[side, 4, 0] + NS - 1) // NS for side in range(2)]
    out_ref[...] = jnp.zeros_like(out_ref)
    amax[...] = jnp.full_like(amax, -jnp.inf)

    def chunk(side, step, s):
        t = step * NS + s
        return meta_ref[side, 3, t]

    def weights(p):
        k = pairs[p] % 8
        for m in range(2):
            w = [rows[k, :, (2 * half + m) * 32:(2 * half + m + 1) * 32, :].reshape(256, 128) for half in range(2)]
            pltpu.matmul_push_rhs(jnp.concatenate(w, axis=1), 0, m, transpose=True)

    def push(side, step, s, half, head=False):
        w = dt[side, chunk(side, step, s)]
        w = [w, jnp.zeros_like(w)]
        w = jnp.concatenate(w[::-1] if half else w, axis=1)
        for m in range(2):
            if head:
                pltpu.matmul_acc_lhs(acc[m][s], w, load_staged_rhs=0)
            else:
                pltpu.matmul_acc_lhs(acc[m][s], w)

    def pop(side, step, s):
        g = chunk(side, step, s) // 8
        for m in range(2):
            r = pltpu.matmul_pop(acc[m][s])
            r = jnp.max(r.reshape(8, 8, 256), axis=0)
            amax[g, m] = jnp.maximum(amax[g, m], r)

    def close(slot, half):
        value = amax[:, 0] + amax[:, 1]
        total[slot] = total[slot] + value if half else value
        amax[...] = jnp.full_like(amax, -jnp.inf)

    @pl.when(count > 0)
    def _():
        weights(0)

        def one_pair(p, state):
            side0, last0, slot0 = state
            slot = pairs[p]
            side = slot // 8
            n = jnp.where(side == 0, steps[0], steps[1])
            for half in range(2):
                for s in range(NS):
                    if half:
                        pop(side, n - 1, s)
                    else:
                        pop(side0, last0, s)
                    push(side, 0, s, half, head=half == 0 and s == 0)
                if half:
                    close(slot, 0)
                else:
                    weights(jnp.minimum(p + 1, count - 1))
                    close(slot0, 1)

                def further(m, _, half=half):
                    for s in range(NS):
                        pop(side, m - 1, s)
                        push(side, m, s, half)
                    return 0

                lax.fori_loop(1, n, further, 0)
            return side, n - 1, slot

        zero = jnp.int32(0)
        side, last, slot = lax.fori_loop(0, count, one_pair, (zero, zero, zero + 16))
        for s in range(NS):
            pop(side, last, s)
        close(slot, 1)
        push(0, 0, 0, 0, head=True)
        pltpu.matmul_pop(acc[0][0])
        pltpu.matmul_pop(acc[1][0])

        def finish(i, _):
            slot = pairs[i]
            sums = total[slot].reshape(128, 256)
            for part in range(2):
                turned = sums[:, part * 128:(part + 1) * 128].T.reshape(4, 4, 8, 128)
                folded = (turned[:, 0] + turned[:, 1]) + (turned[:, 2] + turned[:, 3])
                folded = folded[:, 0:4] + folded[:, 4:8]
                out_ref[slot, pl.ds(part * 16, 16)] = folded.reshape(16, 128)
            return 0

        lax.fori_loop(0, count, finish, 0)


def score(position, pattern, meta, rows, dt):
    smem = pl.BlockSpec(memory_space=pltpu.SMEM)
    vmem = pl.BlockSpec(memory_space=pltpu.VMEM)
    return pl.pallas_call(
        functools.partial(score_kernel, position),
        name="score_blocks",
        out_shape=jax.ShapeDtypeStruct((16, 32, 128), jnp.float32),
        in_specs=[smem, smem, vmem, vmem],
        out_specs=vmem,
        scratch_shapes=[
            pltpu.VMEM((16, 2, 8, 256), jnp.float32),
            pltpu.VMEM((17, 16, 8, 256), jnp.float32),
            pltpu.SMEM((16,), jnp.int32),
        ],
        compiler_params=pltpu.CompilerParams(vmem_limit_bytes=24 << 20),
    )(pattern, meta, rows, dt)


def swap_kernel(part_ref, meta_ref, out_ref, got, s_sem, r_sem):
    idx = lax.axis_index("docs")
    c = idx % 2
    twin = {"docs": idx + 1 - 2 * c, "pb": lax.axis_index("pb")}
    barrier = pltpu.get_barrier_semaphore()
    pl.semaphore_signal(barrier, inc=1, device_id=twin, device_id_type=MESH)
    pl.semaphore_wait(barrier, 1)
    cp = pltpu.make_async_remote_copy(
        src_ref=part_ref.at[pl.ds(8, 8)], dst_ref=got, send_sem=s_sem, recv_sem=r_sem,
        device_id=twin, device_id_type=MESH)
    cp.start()
    rank = jnp.broadcast_to(meta_ref[0, 1:2], (32, 128))

    def place(value, k, core):
        back = jnp.take_along_axis(value, rank, axis=1).reshape(8, 4, 128)
        for h in range(8):
            out_ref[k * 16 + h * 2 + core] = back[h]

    for k in range(8):
        place(part_ref[k], k, c)
    cp.wait_recv()
    for k in range(8):
        place(got[k], k, 1 - c)
    cp.wait_send()


def swap(part, meta):
    vmem = pl.BlockSpec(memory_space=pltpu.VMEM)
    return pl.pallas_call(
        swap_kernel,
        name="swap_scores",
        out_shape=jax.ShapeDtypeStruct((128, 4, 128), jnp.float32),
        in_specs=[vmem, vmem],
        out_specs=vmem,
        scratch_shapes=[
            pltpu.VMEM((8, 32, 128), jnp.float32),
            pltpu.SemaphoreType.DMA,
            pltpu.SemaphoreType.DMA,
        ],
        compiler_params=pltpu.CompilerParams(collective_id=1, has_side_effects=True, vmem_limit_bytes=4 << 20),
    )(part, meta)


def local(queries, documents, lengths, pattern):
    rows, dt, meta = gather(queries, lengths.reshape(1, 128), documents)
    part = score(lambda: lax.axis_index("docs"), pattern, meta, rows.reshape(8, 8, 128, 128), dt)
    return swap(part, meta)


def solution(mesh):
    return jax.shard_map(
        local,
        mesh=mesh,
        in_specs=(P("docs", "pb", None), P("docs", None, None), P("docs"), P()),
        out_specs=P(None, "pb", "docs"),
        check_vma=False,
    )
```

time: 66.9 us -> 50.2 us (0.75)
  the two profiles are of different devices: /device:TPU:117 before, /device:TPU:93 now
where the time goes in v1:
time: 50.2 us; the launch traced here: 50.1 us
  Pallas kernels  49.3 us (98%)
  local copies, waits for them, and re-layouts  0.71 us (1%)
    pallas_call x1, Pallas kernels, gather(): pl.pallas_call(gather_kernel, name='gather_queries', out_shape=(jax.Shape...  22.7 us
    pallas_call x1, Pallas kernels, score(): pl.pallas_call(functools.partial(score_kernel, position), name='score_blo...  21.9 us
    pallas_call x1, Pallas kernels, swap(): pl.pallas_call(swap_kernel, name='swap_scores', out_shape=jax.ShapeDtypeS...  4.75 us

profile of v1, /device:TPU:93, one launch (start us, length us, event | category | flops | bytes accessed | tf_op | source)
XLA Modules:
  0.0 50.1 jit_solution(943584269006614615)
XLA Ops:
  0.0 0.0 copy-start
  0.0 22.7 %gather_queries.1 = (bf16[4,4,4,2,64,128]{5,4,3,2,1,0:T(8,128)(2,1)S(1)}, bf16[2,128,64,128]{3,2,1,0:T(8,128)(2,1)S(1)}, s32[2,8,128]{2,1,0:T(8,128)S(1)}) custom-call(bf16[8,16,128]{2,1,0:T(8,128)(2,1)} %q_hbm.1, s32[1,128]{1,0:T(1,128)} %bitcast.3, bf16[128,64,128]{2,1,0:T(8,128)(2,1)} %d_hbm.1), custom_call_target="tpu_custom_call" | custom-call | tf_op jit(solution)/shard_map/gather_queries/pallas_call | solution.py:184
  22.7 0.0 copy-done
  22.7 21.9 %score_blocks.1.part_ref = f32[16,32,128]{2,1,0:T(8,128)S(1)} custom-call(s32[8,128]{1,0:T(8,128)S(1)} %copy-done, s32[2,8,128]{2,1,0:T(8,128)S(1)} %get-tuple-element.8.refs_1_.meta_ref, bf16[8,8,128,128]{3,2,1,0:T(8,128)(2,1)S(1)} %bitcast.2, bf16[2,128,64,128]{3,2,1,0:T(8,128)(2,1)S(1)} %get-tuple-element.10.refs_3_), custom_call_target="tpu_custom_call" | custom-call | tf_op jit(solution)/shard_map/score_blocks/pallas_call | solution.py:332
  44.6 4.8 %swap_scores.1 = f32[128,4,128]{2,1,0:T(4,128)S(1)} custom-call(f32[16,32,128]{2,1,0:T(8,128)S(1)} %score_blocks.1.part_ref, s32[2,8,128]{2,1,0:T(8,128)S(1)} %get-tuple-element.8.refs_1_.meta_ref), custom_call_target="tpu_custom_call" | custom-call | tf_op jit(solution)/shard_map/swap_scores/pallas_call | solution.py:375
  49.4 0.7 %copy.6 = f32[128,4,128]{2,1,0:T(4,128)} copy(f32[128,4,128]{2,1,0:T(4,128)S(1)} %swap_scores.1) | data formatting | bytes 524288
Async XLA Ops:
  0.0 22.7 %copy-start = (s32[8,128]{1,0:T(8,128)S(1)}, s32[8,128]{1,0:T(8,128)}, u32[]{:S(2)}) copy-start(s32[8,128]{1,0:T(8,128)} %refs_0_.1) | copy-start | bytes 12292

commit v2 on v1

v2 whole, which is shorter than its diff:
```python
import functools

import jax
import jax.numpy as jnp
from jax import lax
from jax.experimental import pallas as pl
from jax.experimental.pallas import tpu as pltpu
from jax.sharding import PartitionSpec as P

MESH = pl.DeviceIdType.MESH
CH = 64
NS = 8


def device(y, zl, x, c, h):
    return {"docs": ((y * 4 + zl) * 4 + x) * 2 + c, "pb": h}


def gather_kernel(q_hbm, len_hbm, d_hbm, q_out, dt_out, meta_out,
                  q_ref, len_ref, tmp, prep, docs, wide, dt, meta, meta_s, zs, zr, ss, sr, ts, tr, ls):
    loads = [pltpu.make_async_copy(src, dst, ls.at[5 + n])
             for n, (src, dst) in enumerate(((q_hbm, q_ref), (len_hbm, len_ref), (d_hbm, docs)))]
    for cp in loads:
        cp.start()
    idx = lax.axis_index("docs")
    zh = lax.axis_index("pb")
    c = idx % 2
    x = (idx // 2) % 4
    zl = (idx // 8) % 4
    y = idx // 32
    z = zh * 4 + zl
    xp, xm, yp, ym = (x + 1) % 4, (x + 3) % 4, (y + 1) % 4, (y + 3) % 4
    x2, y2 = (x + 2) % 4, (y + 2) % 4
    right, left = device(y, zl, xp, c, zh), device(y, zl, xm, c, zh)
    up, down = device(yp, zl, x, c, zh), device(ym, zl, x, c, zh)
    twin = device(y, zl, x, 1 - c, zh)
    column = []
    for s in (4, 3, 5, 2, 6, 1, 7):
        zt = (z + s) % 8
        column.append((zt // 4, device(y, zt % 4, x, c, zt // 4)))

    barrier = pltpu.get_barrier_semaphore()
    for d in [d for _, d in column] + [right, left, up, down, twin]:
        pl.semaphore_signal(barrier, inc=1, device_id=d, device_id_type=MESH)

    loads[0].wait()
    for h in range(2):
        for q in range(4):
            tmp[pl.ds(q, 16, stride=4), :] = q_ref[4 * h + q].astype(jnp.float32)
        prep[h] = tmp[...].astype(jnp.bfloat16)

    loads[1].wait()
    lanes = jnp.broadcast_to(len_ref[...], (128, 128))
    cols = lanes.T
    r = lax.broadcasted_iota(jnp.int32, (128, 128), 0)
    k = lax.broadcasted_iota(jnp.int32, (128, 128), 1)
    rs, ks = jnp.maximum(r - 48, 0) // 16, jnp.maximum(k - 48, 0) // 16
    ahead_col = (ks < rs) | ((ks == rs) & ((lanes > cols) | ((lanes == cols) & (k < r))))
    ahead_row = (rs < ks) | ((rs == ks) & ((cols > lanes) | ((cols == lanes) & (r < k))))
    rank_col = jnp.sum(jnp.where(ahead_col, 1, 0), axis=1, keepdims=True)
    here = rank_col == k
    sizes = jnp.sum(jnp.where(here, cols, 0), axis=0, keepdims=True)
    meta[0:1] = sizes
    meta[1:2] = jnp.sum(jnp.where(ahead_row, 1, 0), axis=0, keepdims=True)
    meta[2:3] = jnp.sum(jnp.where(here, r, 0), axis=0, keepdims=True)
    meta[3:4] = (sizes + 7) // 8
    meta[4:8] = jnp.zeros((4, 128), jnp.int32)
    lm = pltpu.make_async_copy(meta, meta_s, ls.at[2])
    lm.start()
    lm.wait()
    share = []

    pl.semaphore_wait(barrier, 12)

    own = q_out.at[y, zl, x, zh]
    waits = []

    def send(src, dst, s_sem, r_sem, d):
        cp = pltpu.make_async_remote_copy(
            src_ref=src, dst_ref=dst, send_sem=s_sem, recv_sem=r_sem, device_id=d, device_id_type=MESH)
        cp.start()
        waits.append(cp)
        return cp

    first = [send(prep.at[ht], own, zs.at[s], zr.at[s], d) for s, (ht, d) in enumerate(column)]
    lc = pltpu.make_async_copy(prep.at[zh], own, ls.at[1])
    lc.start()

    dests = (right, left, up, down)
    lo = pltpu.make_async_copy(meta, meta_out.at[0], ls.at[3])
    lo.start()
    m0 = send(meta, meta_out.at[1], ts.at[0], tr.at[0], twin)
    for n, d in enumerate(dests):
        share.append(send(meta, meta_out.at[2 + 2 * n], ts.at[6 + n], tr.at[6 + n], d))
    loads[2].wait()

    def arrange(g, _):
        for i in range(8):
            rows = docs[jnp.bitwise_and(meta_s[2, g * 8 + i], 127)].astype(jnp.float32)
            slot = lax.broadcasted_iota(jnp.int32, rows.shape, 0)
            wide[pl.ds(i, 64, stride=8), :] = jnp.where(slot < meta_s[0, g * 8 + i], rows, rows[0:1])
        for i in range(8):
            dt[g * 8 + i] = wide[i * CH:(i + 1) * CH].astype(jnp.bfloat16)
        return 0

    lax.fori_loop(8, 16, arrange, 0)
    for n, d in enumerate(dests):
        share.append(send(dt.at[pl.ds(64 + 16 * n, 16)], dt_out.at[pl.ds(128 + 32 * n, 16)],
                          ts.at[2 + n], tr.at[2 + n], d))
    lax.fori_loop(0, 8, arrange, 0)
    ld = pltpu.make_async_copy(dt.at[pl.ds(0, 64)], dt_out.at[pl.ds(0, 64)], ls.at[4])
    ld.start()
    m1 = send(dt.at[pl.ds(0, 64)], dt_out.at[pl.ds(64, 64)], ts.at[1], tr.at[1], twin)

    lc.wait()
    for cp in first:
        cp.wait_recv()

    a = pl.ds(0, 2)
    b = pl.ds(2, 2)
    used = [0]

    def pass_on(ref, d):
        n = used[0]
        used[0] += 1
        return send(ref, ref, ss.at[n], sr.at[n], d)

    def spread_a(xs):
        return pass_on(q_out.at[y, a, xs], up), pass_on(q_out.at[y, a, xs], down)

    def spread_b(ys):
        return pass_on(q_out.at[ys, b, x], right), pass_on(q_out.at[ys, b, x], left)

    def relay_a(xs, pair):
        pair[0].wait_recv()
        f = pass_on(q_out.at[ym, 0, xs], up)
        pair[1].wait_recv()
        return f, pass_on(q_out.at[yp, 1, xs], down)

    def relay_b(ys, pair):
        pair[0].wait_recv()
        f = pass_on(q_out.at[ys, 2, xm], right)
        pair[1].wait_recv()
        return f, pass_on(q_out.at[ys, 3, xp], left)

    s0 = pass_on(q_out.at[y, a, x], right)
    s1 = pass_on(q_out.at[y, a, x], left)
    s2 = pass_on(q_out.at[y, b, x], up)
    s3 = pass_on(q_out.at[y, b, x], down)
    a0 = spread_a(x)
    b0 = spread_b(y)
    s0.wait_recv()
    s4 = pass_on(q_out.at[y, 0, xm], right)
    s1.wait_recv()
    s5 = pass_on(q_out.at[y, 1, xp], left)
    s2.wait_recv()
    s6 = pass_on(q_out.at[ym, 2, x], up)
    s3.wait_recv()
    s7 = pass_on(q_out.at[yp, 3, x], down)
    for n in range(4):
        share[n].wait_recv()
        m2 = meta_out.at[2 + 2 * n]
        share.append(send(m2, meta_out.at[3 + 2 * n], ts.at[14 + n], tr.at[14 + n], twin))
    a1 = spread_a(xm)
    a2 = spread_a(xp)
    b1 = spread_b(ym)
    b2 = spread_b(yp)
    s4.wait_recv()
    s5.wait_recv()
    a3 = spread_a(x2)
    s6.wait_recv()
    s7.wait_recv()
    b3 = spread_b(y2)
    for n in range(4):
        share[4 + n].wait_recv()
        share.append(send(dt_out.at[pl.ds(128 + 32 * n, 16)], dt_out.at[pl.ds(144 + 32 * n, 16)],
                          ts.at[10 + n], tr.at[10 + n], twin))
    last = share[8:]
    for xs, ys, pa, pb in ((x, y, a0, b0), (xm, ym, a1, b1), (xp, yp, a2, b2), (x2, y2, a3, b3)):
        last.extend(relay_a(xs, pa))
        last.extend(relay_b(ys, pb))
    for cp in [m0, m1] + last:
        cp.wait_recv()
    for cp in (lo, ld):
        cp.wait()
    for cp in waits:
        cp.wait_send()


def gather(queries, lengths, documents):
    hbm = pl.BlockSpec(memory_space=pltpu.HBM)
    free = pl.BlockSpec(memory_space=pl.ANY)
    return pl.pallas_call(
        gather_kernel,
        name="gather_queries",
        out_shape=(
            jax.ShapeDtypeStruct((4, 4, 4, 2, 64, 128), jnp.bfloat16),
            jax.ShapeDtypeStruct((256, CH, 128), jnp.bfloat16),
            jax.ShapeDtypeStruct((10, 8, 128), jnp.int32),
        ),
        in_specs=[hbm, hbm, hbm],
        out_specs=(free, free, free),
        scratch_shapes=[
            pltpu.VMEM((8, 16, 128), jnp.bfloat16),
            pltpu.VMEM((1, 128), jnp.int32),
            pltpu.VMEM((64, 128), jnp.float32),
            pltpu.VMEM((2, 64, 128), jnp.bfloat16),
            pltpu.VMEM((128, 64, 128), jnp.bfloat16),
            pltpu.VMEM((512, 128), jnp.float32),
            pltpu.VMEM((128, CH, 128), jnp.bfloat16),
            pltpu.VMEM((8, 128), jnp.int32),
            pltpu.SMEM((8, 128), jnp.int32),
            pltpu.SemaphoreType.DMA((7,)),
            pltpu.SemaphoreType.DMA((7,)),
            pltpu.SemaphoreType.DMA((40,)),
            pltpu.SemaphoreType.DMA((40,)),
            pltpu.SemaphoreType.DMA((18,)),
            pltpu.SemaphoreType.DMA((18,)),
            pltpu.SemaphoreType.DMA((8,)),
        ],
        compiler_params=pltpu.CompilerParams(collective_id=0, has_side_effects=True, vmem_limit_bytes=12 << 20),
    )(*[pltpu.with_memory_space_constraint(v, pltpu.HBM) for v in (queries, lengths, documents)])


def score_kernel(position, *refs):
    pl.run_scoped(
        functools.partial(score_body, position, *refs),
        *([pltpu.ACC(0)((CH, 256), jnp.float32)] * NS + [pltpu.ACC(1)((CH, 256), jnp.float32)] * NS),
    )


def around(idx):
    c, x, zl, y = idx % 2, (idx // 2) % 4, (idx // 8) % 4, idx // 32

    def at(y, x, c):
        return ((y * 4 + zl) * 4 + x) * 2 + c

    xp, xm, yp, ym = (x + 1) % 4, (x + 3) % 4, (y + 1) % 4, (y + 3) % 4
    return c, [[at(v, u, w) for w in (c, 1 - c)] for v, u in ((y, xm), (y, xp), (ym, x), (yp, x))]


def score_body(position, pat_ref, meta_ref, rows, dt, out_ref, amax, total, stage, lists, steps, blocks, *accs):
    acc = (accs[:NS], accs[NS:])
    idx = position()
    c, near = around(idx)
    sides = [(idx, 0, 8, 0, 0), (idx + 1 - 2 * c, 8, 8, 1, 0)]
    for n in range(4):
        for o in range(2):
            sides.append((near[n][o], 16 + 4 * n + 2 * o, 2, 2 + 2 * n + o, 8 + 2 * n))

    def listing(k, n):
        t = jnp.int32(0)
        for col, here, groups, table, there in sides:
            def add(t, here=here, groups=groups, table=table, there=there):
                for g in range(groups):
                    for i in range(8):
                        lists[n, t + i] = (here + g) * 8 + i
                    t = t + meta_ref[table, 3, (there + g) * 8]
                return t

            t = lax.cond(pat_ref[k, col] > 0, add, lambda t: t, t)

        @pl.when(t > 0)
        def _():
            end = lists[n, t - 1]
            for i in range(NS):
                lists[n, t + i] = end
            steps[n] = jnp.right_shift(t + NS - 1, 3)
            blocks[n] = k

        return n + (t > 0).astype(jnp.int32)

    count = lax.fori_loop(0, 8, listing, jnp.int32(0))
    stage[...] = jnp.zeros_like(stage)
    amax[...] = jnp.full_like(amax, -jnp.inf)

    def weights(p):
        k = blocks[p]
        for m in range(2):
            w = [rows[k, :, (2 * half + m) * 32:(2 * half + m + 1) * 32, :].reshape(256, 128) for half in range(2)]
            pltpu.matmul_push_rhs(jnp.concatenate(w, axis=1), 0, m, transpose=True)

    def push(at, half, s, head=False):
        w = dt[at]
        w = [w, jnp.zeros_like(w)]
        w = jnp.concatenate(w[::-1] if half else w, axis=1)
        for m in range(2):
            if head:
                pltpu.matmul_acc_lhs(acc[m][s], w, load_staged_rhs=0)
            else:
                pltpu.matmul_acc_lhs(acc[m][s], w)

    def pop(at, s):
        g = jnp.right_shift(at, 3)
        for m in range(2):
            r = pltpu.matmul_pop(acc[m][s])
            r = jnp.max(r.reshape(8, 8, 256), axis=0)
            amax[g, m] = jnp.maximum(amax[g, m], r)

    def close(p, half):
        value = amax[:, 0] + amax[:, 1]
        total[p] = total[p] + value if half else value
        amax[...] = jnp.full_like(amax, -jnp.inf)

    @pl.when(count > 0)
    def _():
        weights(0)

        def one_block(p, state):
            p0, last0 = state
            n = steps[p]
            for half in range(2):
                before = (p, n - 1) if half else (jnp.maximum(p0, 0), last0)
                olds = [lists[before[0], before[1] * NS + s] for s in range(NS)]
                news = [lists[p, s] for s in range(NS)]
                for s in range(NS):
                    pop(olds[s], s)
                    push(news[s], half, s, head=half == 0 and s == 0)
                if half:
                    close(p, 0)
                else:
                    weights(jnp.minimum(p + 1, count - 1))
                    close(jnp.where(p0 < 0, 8, p0), 1)

                def further(m, _, half=half):
                    olds = [lists[p, (m - 1) * NS + s] for s in range(NS)]
                    news = [lists[p, m * NS + s] for s in range(NS)]
                    for s in range(NS):
                        pop(olds[s], s)
                        push(news[s], half, s)
                    return 0

                lax.fori_loop(1, n, further, 0)
            return p, n - 1

        zero = jnp.int32(0)
        p, last = lax.fori_loop(0, count, one_block, (zero - 1, zero))
        for s in range(NS):
            pop(lists[p, last * NS + s], s)
        close(p, 1)
        push(0, 0, 0, head=True)
        pltpu.matmul_pop(acc[0][0])
        pltpu.matmul_pop(acc[1][0])

        lane = lax.broadcasted_iota(jnp.int32, (32, 128), 1)

        def finish(p, _):
            k = blocks[p]
            flags = [pat_ref[k, side[0]] for side in sides]
            for part in range(2):
                on = jnp.zeros((32, 128), jnp.int32)
                for flag, (_, here, groups, _, _) in zip(flags, sides):
                    if here // 16 == part:
                        low = (here % 16) * 8
                        on = jnp.where((lane >= low) & (lane < low + groups * 8), flag, on)
                sums = total[p, part * 16:(part + 1) * 16].reshape(128, 256)
                for h in range(2):
                    turned = sums[:, h * 128:(h + 1) * 128].T.reshape(4, 4, 8, 128)
                    folded = (turned[:, 0] + turned[:, 1]) + (turned[:, 2] + turned[:, 3])
                    folded = (folded[:, 0:4] + folded[:, 4:8]).reshape(16, 128)
                    stage[k // 4, pl.ds(pl.multiple_of((k % 4) * 32 + h * 16, 16), 16), part * 128:(part + 1) * 128] = (
                        jnp.where(on[:16] > 0, folded, 0.0))
            return 0

        lax.fori_loop(0, count, finish, 0)

    for side in range(2):
        for part in range(2):
            out_ref[side, part * 128:(part + 1) * 128] = stage[side, :, part * 128:(part + 1) * 128].T


def score(position, pattern, meta, rows, dt):
    smem = pl.BlockSpec(memory_space=pltpu.SMEM)
    vmem = pl.BlockSpec(memory_space=pltpu.VMEM)
    return pl.pallas_call(
        functools.partial(score_kernel, position),
        name="score_blocks",
        out_shape=jax.ShapeDtypeStruct((2, 256, 128), jnp.float32),
        in_specs=[smem, smem, vmem, vmem],
        out_specs=vmem,
        scratch_shapes=[
            pltpu.VMEM((32, 2, 8, 256), jnp.float32),
            pltpu.VMEM((9, 32, 8, 256), jnp.float32),
            pltpu.VMEM((2, 128, 256), jnp.float32),
            pltpu.SMEM((8, 256 + NS), jnp.int32),
            pltpu.SMEM((8,), jnp.int32),
            pltpu.SMEM((8,), jnp.int32),
        ],
        compiler_params=pltpu.CompilerParams(vmem_limit_bytes=24 << 20),
    )(pattern, meta, rows, dt)


def swap_kernel(part_ref, meta_ref, out_ref, got, s_sem, r_sem):
    idx = lax.axis_index("docs")
    zh = lax.axis_index("pb")
    c, near = around(idx)
    twin = {"docs": idx + 1 - 2 * c, "pb": zh}
    partners = [{"docs": near[n][o], "pb": zh} for n in range(4) for o in range(2)]
    barrier = pltpu.get_barrier_semaphore()
    for d in partners + [twin]:
        pl.semaphore_signal(barrier, inc=1, device_id=d, device_id_type=MESH)
    pl.semaphore_wait(barrier, 9)
    copies = []
    for n in range(4):
        for o in range(2):
            q = 2 * n + o
            copies.append(pltpu.make_async_remote_copy(
                src_ref=part_ref.at[:, pl.ds(128 + 16 * q, 16)], dst_ref=got.at[c, :, pl.ds(64 + 16 * n, 16)],
                send_sem=s_sem.at[q], recv_sem=r_sem.at[q], device_id=partners[q], device_id_type=MESH))
    copies.append(pltpu.make_async_remote_copy(
        src_ref=part_ref.at[:, pl.ds(64, 64)], dst_ref=got.at[c, :, pl.ds(0, 64)],
        send_sem=s_sem.at[8], recv_sem=r_sem.at[8], device_id=twin, device_id_type=MESH))
    for cp in copies:
        cp.start()
    got[c, :, 0:64] = part_ref[:, 0:64]
    rank = jnp.broadcast_to(meta_ref[0, 1:2], (128, 128))
    for cp in copies:
        cp.wait_recv()
    for core in range(2):
        for half in range(2):
            back = jnp.take_along_axis(got[core, half].T, rank, axis=1).reshape(4, 8, 4, 128)
            for k in range(4):
                for h in range(8):
                    out_ref[(half * 4 + k) * 16 + h * 2 + core] = back[k, h]
    for cp in copies:
        cp.wait_send()


def swap(part, meta):
    vmem = pl.BlockSpec(memory_space=pltpu.VMEM)
    return pl.pallas_call(
        swap_kernel,
        name="swap_scores",
        out_shape=jax.ShapeDtypeStruct((128, 4, 128), jnp.float32),
        in_specs=[vmem, vmem],
        out_specs=vmem,
        scratch_shapes=[
            pltpu.VMEM((2, 2, 128, 128), jnp.float32),
            pltpu.SemaphoreType.DMA((9,)),
            pltpu.SemaphoreType.DMA((9,)),
        ],
        compiler_params=pltpu.CompilerParams(collective_id=1, has_side_effects=True, vmem_limit_bytes=4 << 20),
    )(part, meta)


def local(queries, documents, lengths, pattern):
    rows, dt, meta = gather(queries, lengths.reshape(1, 128), documents)
    part = score(lambda: lax.axis_index("docs"), pattern, meta, rows.reshape(8, 8, 128, 128), dt)
    return swap(part, meta)


def solution(mesh):
    return jax.shard_map(
        local,
        mesh=mesh,
        in_specs=(P("docs", "pb", None), P("docs", None, None), P("docs"), P()),
        out_specs=P(None, "pb", "docs"),
        check_vma=False,
    )
```

time: 50.2 us -> 60.5 us (1.21)
  the two profiles are of different devices: /device:TPU:93 before, /device:TPU:1 now
where the time goes in v2:
time: 60.5 us; the launch traced here: 60.4 us
  Pallas kernels  59.7 us (99%)
  local copies, waits for them, and re-layouts  0.71 us (1%)
    pallas_call x1, Pallas kernels, gather(): pl.pallas_call(gather_kernel, name='gather_queries', out_shape=(jax.Shape...  30.8 us
    pallas_call x1, Pallas kernels, score(): pl.pallas_call(functools.partial(score_kernel, position), name='score_blo...  16 us
    pallas_call x1, Pallas kernels, swap(): pl.pallas_call(swap_kernel, name='swap_scores', out_shape=jax.ShapeDtypeS...  12.8 us

profile of v2, /device:TPU:1, one launch (start us, length us, event | category | flops | bytes accessed | tf_op | source)
XLA Modules:
  0.0 60.4 jit_solution(8304276450894150368)
XLA Ops:
  0.0 0.0 copy-start
  0.0 30.8 %gather_queries.1 = (bf16[4,4,4,2,64,128]{5,4,3,2,1,0:T(8,128)(2,1)S(1)}, bf16[256,64,128]{2,1,0:T(8,128)(2,1)S(1)}, s32[10,8,128]{2,1,0:T(8,128)S(1)}) custom-call(bf16[8,16,128]{2,1,0:T(8,128)(2,1)} %q_hbm.1, s32[1,128]{1,0:T(1,128)} %bitcast.3, bf16[128,64,128]{2,1,0:T(8,128)(2,1)} %d_hbm.1), custom_call_target="tpu_custom_call" | custom-call | tf_op jit(solution)/shard_map/gather_queries/pallas_call | solution.py:193
  30.8 0.0 copy-done
  30.8 16.0 %score_blocks.1.part_ref = f32[2,256,128]{2,1,0:T(8,128)S(1)} custom-call(s32[8,128]{1,0:T(8,128)S(1)} %copy-done, s32[10,8,128]{2,1,0:T(8,128)S(1)} %get-tuple-element.8.refs_1_.meta_ref, bf16[8,8,128,128]{3,2,1,0:T(8,128)(2,1)S(1)} %bitcast.2, bf16[256,64,128]{2,1,0:T(8,128)(2,1)S(1)} %get-tuple-element.10.refs_3_), custom_call_target="tpu_custom_call" | custom-call | tf_op jit(solution)/shard_map/score_blocks/pallas_call | solution.py:375
  46.9 12.8 %swap_scores.1 = f32[128,4,128]{2,1,0:T(4,128)S(1)} custom-call(f32[2,256,128]{2,1,0:T(8,128)S(1)} %score_blocks.1.part_ref, s32[10,8,128]{2,1,0:T(8,128)S(1)} %get-tuple-element.8.refs_1_.meta_ref), custom_call_target="tpu_custom_call" | custom-call | tf_op jit(solution)/shard_map/swap_scores/pallas_call | solution.py:431
  59.7 0.7 %copy.6 = f32[128,4,128]{2,1,0:T(4,128)} copy(f32[128,4,128]{2,1,0:T(4,128)S(1)} %swap_scores.1) | data formatting | bytes 524288
Async XLA Ops:
  0.0 30.8 %copy-start = (s32[8,128]{1,0:T(8,128)S(1)}, s32[8,128]{1,0:T(8,128)}, u32[]{:S(2)}) copy-start(s32[8,128]{1,0:T(8,128)} %refs_0_.1) | copy-start | bytes 12292

commit v3 on v2

--- a/solution.py
+++ b/solution.py
@@ -9,7 +9,8 @@
 
 MESH = pl.DeviceIdType.MESH
 CH = 64
-NS = 8
+NS = 12
+RUN = NS // 2
 
 
 def device(y, zl, x, c, h):
@@ -69,29 +70,6 @@
     lm.start()
     lm.wait()
     share = []
-
-    pl.semaphore_wait(barrier, 12)
-
-    own = q_out.at[y, zl, x, zh]
-    waits = []
-
-    def send(src, dst, s_sem, r_sem, d):
-        cp = pltpu.make_async_remote_copy(
-            src_ref=src, dst_ref=dst, send_sem=s_sem, recv_sem=r_sem, device_id=d, device_id_type=MESH)
-        cp.start()
-        waits.append(cp)
-        return cp
-
-    first = [send(prep.at[ht], own, zs.at[s], zr.at[s], d) for s, (ht, d) in enumerate(column)]
-    lc = pltpu.make_async_copy(prep.at[zh], own, ls.at[1])
-    lc.start()
-
-    dests = (right, left, up, down)
-    lo = pltpu.make_async_copy(meta, meta_out.at[0], ls.at[3])
-    lo.start()
-    m0 = send(meta, meta_out.at[1], ts.at[0], tr.at[0], twin)
-    for n, d in enumerate(dests):
-        share.append(send(meta, meta_out.at[2 + 2 * n], ts.at[6 + n], tr.at[6 + n], d))
     loads[2].wait()
 
     def arrange(g, _):
@@ -104,6 +82,28 @@
         return 0
 
     lax.fori_loop(8, 16, arrange, 0)
+    pl.semaphore_wait(barrier, 12)
+
+    own = q_out.at[y, zl, x, zh]
+    waits = []
+
+    def send(src, dst, s_sem, r_sem, d):
+        cp = pltpu.make_async_remote_copy(
+            src_ref=src, dst_ref=dst, send_sem=s_sem, recv_sem=r_sem, device_id=d, device_id_type=MESH)
+        cp.start()
+        waits.append(cp)
+        return cp
+
+    first = [send(prep.at[ht], own, zs.at[s], zr.at[s], d) for s, (ht, d) in enumerate(column)]
+    lc = pltpu.make_async_copy(prep.at[zh], own, ls.at[1])
+    lc.start()
+
+    dests = (right, left, up, down)
+    lo = pltpu.make_async_copy(meta, meta_out.at[0], ls.at[3])
+    lo.start()
+    m0 = send(meta, meta_out.at[1], ts.at[0], tr.at[0], twin)
+    for n, d in enumerate(dests):
+        share.append(send(meta, meta_out.at[2 + 2 * n], ts.at[6 + n], tr.at[6 + n], d))
     for n, d in enumerate(dests):
         share.append(send(dt.at[pl.ds(64 + 16 * n, 16)], dt_out.at[pl.ds(128 + 32 * n, 16)],
                           ts.at[2 + n], tr.at[2 + n], d))
@@ -263,84 +263,88 @@
         @pl.when(t > 0)
         def _():
             end = lists[n, t - 1]
-            for i in range(NS):
+            for i in range(RUN):
                 lists[n, t + i] = end
-            steps[n] = jnp.right_shift(t + NS - 1, 3)
+            steps[n] = (t + RUN - 1) // RUN
             blocks[n] = k
 
         return n + (t > 0).astype(jnp.int32)
 
     count = lax.fori_loop(0, 8, listing, jnp.int32(0))
     stage[...] = jnp.zeros_like(stage)
-    amax[...] = jnp.full_like(amax, -jnp.inf)
 
     def weights(p):
         k = blocks[p]
         for m in range(2):
-            w = [rows[k, :, (2 * half + m) * 32:(2 * half + m + 1) * 32, :].reshape(256, 128) for half in range(2)]
+            w = []
+            for half in range(2):
+                low = (2 * half + m) * 32
+                w.append(jnp.concatenate([rows[k, :, low + 16 * t:low + 16 * t + 16, :].reshape(128, 128) for t in range(2)], axis=0))
             pltpu.matmul_push_rhs(jnp.concatenate(w, axis=1), 0, m, transpose=True)
 
-    def push(at, half, s, head=False):
+    def push(at, s, head=False):
         w = dt[at]
-        w = [w, jnp.zeros_like(w)]
-        w = jnp.concatenate(w[::-1] if half else w, axis=1)
-        for m in range(2):
-            if head:
-                pltpu.matmul_acc_lhs(acc[m][s], w, load_staged_rhs=0)
-            else:
-                pltpu.matmul_acc_lhs(acc[m][s], w)
-
-    def pop(at, s):
+        for half in range(2):
+            v = [w, jnp.zeros_like(w)]
+            v = jnp.concatenate(v[::-1] if half else v, axis=1)
+            for m in range(2):
+                if head and half == 0:
+                    pltpu.matmul_acc_lhs(acc[m][2 * s], v, load_staged_rhs=0)
+                else:
+                    pltpu.matmul_acc_lhs(acc[m][2 * s + half], v)
+
+    def pop(at, s, tops):
         g = jnp.right_shift(at, 3)
-        for m in range(2):
-            r = pltpu.matmul_pop(acc[m][s])
-            r = jnp.max(r.reshape(8, 8, 256), axis=0)
-            amax[g, m] = jnp.maximum(amax[g, m], r)
-
-    def close(p, half):
-        value = amax[:, 0] + amax[:, 1]
-        total[p] = total[p] + value if half else value
-        amax[...] = jnp.full_like(amax, -jnp.inf)
+        roof = jnp.where(jnp.bitwise_and(at, 7) == 0, -jnp.inf, jnp.inf).astype(jnp.float32)
+        after = []
+        for half in range(2):
+            for m in range(2):
+                r = pltpu.matmul_pop(acc[m][2 * s + half])
+                r = jnp.max(r.reshape(8, 8, 256), axis=0)
+                r = jnp.maximum(jnp.minimum(tops[2 * half + m], roof), r)
+                amax[g, 2 * half + m] = r
+                after.append(r)
+        return after
+
+    def close(p):
+        value = (amax[:, 0] + amax[:, 1]) + (amax[:, 2] + amax[:, 3])
+        total[p] = value[:, :, :128] + value[:, :, 128:]
 
     @pl.when(count > 0)
     def _():
         weights(0)
 
         def one_block(p, state):
-            p0, last0 = state
+            p0, last0, tops = state
             n = steps[p]
-            for half in range(2):
-                before = (p, n - 1) if half else (jnp.maximum(p0, 0), last0)
-                olds = [lists[before[0], before[1] * NS + s] for s in range(NS)]
-                news = [lists[p, s] for s in range(NS)]
-                for s in range(NS):
-                    pop(olds[s], s)
-                    push(news[s], half, s, head=half == 0 and s == 0)
-                if half:
-                    close(p, 0)
-                else:
-                    weights(jnp.minimum(p + 1, count - 1))
-                    close(jnp.where(p0 < 0, 8, p0), 1)
-
-                def further(m, _, half=half):
-                    olds = [lists[p, (m - 1) * NS + s] for s in range(NS)]
-                    news = [lists[p, m * NS + s] for s in range(NS)]
-                    for s in range(NS):
-                        pop(olds[s], s)
-                        push(news[s], half, s)
-                    return 0
-
-                lax.fori_loop(1, n, further, 0)
-            return p, n - 1
+            olds = [lists[jnp.maximum(p0, 0), last0 * RUN + s] for s in range(RUN)]
+            news = [lists[p, s] for s in range(RUN)]
+            for s in range(RUN):
+                tops = pop(olds[s], s, tops)
+                push(news[s], s, head=s == 0)
+            weights(jnp.minimum(p + 1, count - 1))
+            close(jnp.where(p0 < 0, 8, p0))
+
+            def further(m, tops):
+                olds = [lists[p, (m - 1) * RUN + s] for s in range(RUN)]
+                news = [lists[p, m * RUN + s] for s in range(RUN)]
+                for s in range(RUN):
+                    tops = pop(olds[s], s, tops)
+                    push(news[s], s)
+                return tops
+
+            return p, n - 1, lax.fori_loop(1, n, further, tops)
 
         zero = jnp.int32(0)
-        p, last = lax.fori_loop(0, count, one_block, (zero - 1, zero))
-        for s in range(NS):
-            pop(lists[p, last * NS + s], s)
-        close(p, 1)
-        push(0, 0, 0, head=True)
-        pltpu.matmul_pop(acc[0][0])
-        pltpu.matmul_pop(acc[1][0])
+        start = [jnp.full((8, 256), -jnp.inf, jnp.float32)] * 4
+        p, last, tops = lax.fori_loop(0, count, one_block, (zero - 1, zero, start))
+        for s in range(RUN):
+            tops = pop(lists[p, last * RUN + s], s, tops)
+        close(p)
+        push(0, 0, head=True)
+        for half in range(2):
+            for m in range(2):
+                pltpu.matmul_pop(acc[m][half])
 
         lane = lax.broadcasted_iota(jnp.int32, (32, 128), 1)
 
@@ -353,13 +357,11 @@
                     if here // 16 == part:
                         low = (here % 16) * 8
                         on = jnp.where((lane >= low) & (lane < low + groups * 8), flag, on)
-                sums = total[p, part * 16:(part + 1) * 16].reshape(128, 256)
-                for h in range(2):
-                    turned = sums[:, h * 128:(h + 1) * 128].T.reshape(4, 4, 8, 128)
-                    folded = (turned[:, 0] + turned[:, 1]) + (turned[:, 2] + turned[:, 3])
-                    folded = (folded[:, 0:4] + folded[:, 4:8]).reshape(16, 128)
-                    stage[k // 4, pl.ds(pl.multiple_of((k % 4) * 32 + h * 16, 16), 16), part * 128:(part + 1) * 128] = (
-                        jnp.where(on[:16] > 0, folded, 0.0))
+                turned = total[p, part * 16:(part + 1) * 16].reshape(128, 128).T.reshape(8, 2, 8, 128)
+                folded = turned[:, 0] + turned[:, 1]
+                folded = (folded[:, 0:4] + folded[:, 4:8]).reshape(32, 128)
+                stage[k // 4, pl.ds(pl.multiple_of((k % 4) * 32, 32), 32), part * 128:(part + 1) * 128] = (
+                    jnp.where(on > 0, folded, 0.0))
             return 0
 
         lax.fori_loop(0, count, finish, 0)
@@ -379,8 +381,8 @@
         in_specs=[smem, smem, vmem, vmem],
         out_specs=vmem,
         scratch_shapes=[
-            pltpu.VMEM((32, 2, 8, 256), jnp.float32),
-            pltpu.VMEM((9, 32, 8, 256), jnp.float32),
+            pltpu.VMEM((32, 4, 8, 256), jnp.float32),
+            pltpu.VMEM((9, 32, 8, 128), jnp.float32),
             pltpu.VMEM((2, 128, 256), jnp.float32),
             pltpu.SMEM((8, 256 + NS), jnp.int32),
             pltpu.SMEM((8,), jnp.int32),

time: 60.5 us -> 57.9 us (0.957)
  the two profiles are of different devices: /device:TPU:1 before, /device:TPU:65 now
where the time goes in v3:
time: 57.9 us; the launch traced here: 57.8 us
  Pallas kernels  57 us (98%)
  local copies, waits for them, and re-layouts  0.71 us (1%)
    pallas_call x1, Pallas kernels, gather(): pl.pallas_call(gather_kernel, name='gather_queries', out_shape=(jax.Shape...  27.4 us
    pallas_call x1, Pallas kernels, score(): pl.pallas_call(functools.partial(score_kernel, position), name='score_blo...  15 us
    pallas_call x1, Pallas kernels, swap(): pl.pallas_call(swap_kernel, name='swap_scores', out_shape=jax.ShapeDtypeS...  14.6 us

profile of v3, /device:TPU:65, one launch (start us, length us, event | category | flops | bytes accessed | tf_op | source)
XLA Modules:
  0.0 57.8 jit_solution(6219829192082565496)
XLA Ops:
  0.0 0.0 copy-start
  0.0 27.4 %gather_queries.1 = (bf16[4,4,4,2,64,128]{5,4,3,2,1,0:T(8,128)(2,1)S(1)}, bf16[256,64,128]{2,1,0:T(8,128)(2,1)S(1)}, s32[10,8,128]{2,1,0:T(8,128)S(1)}) custom-call(bf16[8,16,128]{2,1,0:T(8,128)(2,1)} %q_hbm.1, s32[1,128]{1,0:T(1,128)} %bitcast.3, bf16[128,64,128]{2,1,0:T(8,128)(2,1)} %d_hbm.1), custom_call_target="tpu_custom_call" | custom-call | tf_op jit(solution)/shard_map/gather_queries/pallas_call | solution.py:193
  27.4 0.0 copy-done
  27.4 15.0 %score_blocks.1.part_ref = f32[2,256,128]{2,1,0:T(8,128)S(1)} custom-call(s32[8,128]{1,0:T(8,128)S(1)} %copy-done, s32[10,8,128]{2,1,0:T(8,128)S(1)} %get-tuple-element.8.refs_1_.meta_ref, bf16[8,8,128,128]{3,2,1,0:T(8,128)(2,1)S(1)} %bitcast.2, bf16[256,64,128]{2,1,0:T(8,128)(2,1)S(1)} %get-tuple-element.10.refs_3_), custom_call_target="tpu_custom_call" | custom-call | tf_op jit(solution)/shard_map/score_blocks/pallas_call | solution.py:377
  42.5 14.6 %swap_scores.1 = f32[128,4,128]{2,1,0:T(4,128)S(1)} custom-call(f32[2,256,128]{2,1,0:T(8,128)S(1)} %score_blocks.1.part_ref, s32[10,8,128]{2,1,0:T(8,128)S(1)} %get-tuple-element.8.refs_1_.meta_ref), custom_call_target="tpu_custom_call" | custom-call | tf_op jit(solution)/shard_map/swap_scores/pallas_call | solution.py:433
  57.1 0.7 %copy.6 = f32[128,4,128]{2,1,0:T(4,128)} copy(f32[128,4,128]{2,1,0:T(4,128)S(1)} %swap_scores.1) | data formatting | bytes 524288
Async XLA Ops:
  0.0 27.4 %copy-start = (s32[8,128]{1,0:T(8,128)S(1)}, s32[8,128]{1,0:T(8,128)}, u32[]{:S(2)}) copy-start(s32[8,128]{1,0:T(8,128)} %refs_0_.1) | copy-start | bytes 12292

commit v4 on v3

--- a/solution.py
+++ b/solution.py
@@ -15,6 +15,17 @@
 
 def device(y, zl, x, c, h):
     return {"docs": ((y * 4 + zl) * 4 + x) * 2 + c, "pb": h}
+
+
+SHARES = (0, 2, 4, 6, 9, 11, 13, 15, 1, 14, 3, 12, 5, 10, 7, 8)
+
+
+def placed(rank):
+    group = rank // 8
+    slot = jnp.zeros_like(rank)
+    for n, g in enumerate(SHARES):
+        slot = jnp.where(group == g, n, slot)
+    return slot * 8 + rank % 8
 
 
 def gather_kernel(q_hbm, len_hbm, d_hbm, q_out, dt_out, meta_out,
@@ -55,14 +66,14 @@
     cols = lanes.T
     r = lax.broadcasted_iota(jnp.int32, (128, 128), 0)
     k = lax.broadcasted_iota(jnp.int32, (128, 128), 1)
-    rs, ks = jnp.maximum(r - 48, 0) // 16, jnp.maximum(k - 48, 0) // 16
-    ahead_col = (ks < rs) | ((ks == rs) & ((lanes > cols) | ((lanes == cols) & (k < r))))
-    ahead_row = (rs < ks) | ((rs == ks) & ((cols > lanes) | ((cols == lanes) & (r < k))))
-    rank_col = jnp.sum(jnp.where(ahead_col, 1, 0), axis=1, keepdims=True)
+    ahead_col = (lanes > cols) | ((lanes == cols) & (k < r))
+    ahead_row = (cols > lanes) | ((cols == lanes) & (r < k))
+    rank_col = placed(jnp.sum(jnp.where(ahead_col, 1, 0), axis=1, keepdims=True))
+    rank_row = placed(jnp.sum(jnp.where(ahead_row, 1, 0), axis=0, keepdims=True))
     here = rank_col == k
     sizes = jnp.sum(jnp.where(here, cols, 0), axis=0, keepdims=True)
     meta[0:1] = sizes
-    meta[1:2] = jnp.sum(jnp.where(ahead_row, 1, 0), axis=0, keepdims=True)
+    meta[1:2] = rank_row
     meta[2:3] = jnp.sum(jnp.where(here, r, 0), axis=0, keepdims=True)
     meta[3:4] = (sizes + 7) // 8
     meta[4:8] = jnp.zeros((4, 128), jnp.int32)
@@ -239,8 +250,11 @@
     return c, [[at(v, u, w) for w in (c, 1 - c)] for v, u in ((y, xm), (y, xp), (ym, x), (yp, x))]
 
 
-def score_body(position, pat_ref, meta_ref, rows, dt, out_ref, amax, total, stage, lists, steps, blocks, *accs):
+def score_body(position, pat_ref, meta_vmem, rows, dt, out_ref, amax, total, stage, lists, steps, blocks, needs, sem, *accs):
     acc = (accs[:NS], accs[NS:])
+    copy = pltpu.make_async_copy(meta_vmem.at[:, pl.ds(3, 1)], needs, sem)
+    copy.start()
+    stage[...] = jnp.zeros_like(stage)
     idx = position()
     c, near = around(idx)
     sides = [(idx, 0, 8, 0, 0), (idx + 1 - 2 * c, 8, 8, 1, 0)]
@@ -255,7 +269,7 @@
                 for g in range(groups):
                     for i in range(8):
                         lists[n, t + i] = (here + g) * 8 + i
-                    t = t + meta_ref[table, 3, (there + g) * 8]
+                    t = t + needs[table, 0, (there + g) * 8]
                 return t
 
             t = lax.cond(pat_ref[k, col] > 0, add, lambda t: t, t)
@@ -270,8 +284,8 @@
 
         return n + (t > 0).astype(jnp.int32)
 
+    copy.wait()
     count = lax.fori_loop(0, 8, listing, jnp.int32(0))
-    stage[...] = jnp.zeros_like(stage)
 
     def weights(p):
         k = blocks[p]
@@ -378,7 +392,7 @@
         functools.partial(score_kernel, position),
         name="score_blocks",
         out_shape=jax.ShapeDtypeStruct((2, 256, 128), jnp.float32),
-        in_specs=[smem, smem, vmem, vmem],
+        in_specs=[smem, vmem, vmem, vmem],
         out_specs=vmem,
         scratch_shapes=[
             pltpu.VMEM((32, 4, 8, 256), jnp.float32),
@@ -387,6 +401,8 @@
             pltpu.SMEM((8, 256 + NS), jnp.int32),
             pltpu.SMEM((8,), jnp.int32),
             pltpu.SMEM((8,), jnp.int32),
+            pltpu.SMEM((10, 1, 128), jnp.int32),
+            pltpu.SemaphoreType.DMA,
         ],
         compiler_params=pltpu.CompilerParams(vmem_limit_bytes=24 << 20),
     )(pattern, meta, rows, dt)

time: 57.9 us -> 57.3 us (0.990)
  the two profiles are of different devices: /device:TPU:65 before, /device:TPU:33 now
where the time goes in v4:
time: 57.3 us; the launch traced here: 57.2 us
  Pallas kernels  56.5 us (99%)
  local copies, waits for them, and re-layouts  0.71 us (1%)
    pallas_call x1, Pallas kernels, gather(): pl.pallas_call(gather_kernel, name='gather_queries', out_shape=(jax.Shape...  28.3 us
    pallas_call x1, Pallas kernels, swap(): pl.pallas_call(swap_kernel, name='swap_scores', out_shape=jax.ShapeDtypeS...  18.4 us
    pallas_call x1, Pallas kernels, score(): pl.pallas_call(functools.partial(score_kernel, position), name='score_blo...  9.71 us

profile of v4, /device:TPU:33, one launch (start us, length us, event | category | flops | bytes accessed | tf_op | source)
XLA Modules:
  0.0 57.2 jit_solution(14516181182527623600)
XLA Ops:
  0.0 0.0 copy-start
  0.0 28.3 %gather_queries.1 = (bf16[4,4,4,2,64,128]{5,4,3,2,1,0:T(8,128)(2,1)S(1)}, bf16[256,64,128]{2,1,0:T(8,128)(2,1)S(1)}, s32[10,8,128]{2,1,0:T(8,128)S(1)}) custom-call(bf16[8,16,128]{2,1,0:T(8,128)(2,1)} %q_hbm.1, s32[1,128]{1,0:T(1,128)} %bitcast.3, bf16[128,64,128]{2,1,0:T(8,128)(2,1)} %d_hbm.1), custom_call_target="tpu_custom_call" | custom-call | tf_op jit(solution)/shard_map/gather_queries/pallas_call | solution.py:204
  28.3 0.0 copy-done
  28.3 9.7 %score_blocks.1.part_ref = f32[2,256,128]{2,1,0:T(8,128)S(1)} custom-call(s32[8,128]{1,0:T(8,128)S(1)} %copy-done, s32[10,8,128]{2,1,0:T(8,128)S(1)} %get-tuple-element.8.refs_1_.meta_ref, bf16[8,8,128,128]{3,2,1,0:T(8,128)(2,1)S(1)} %bitcast.2, bf16[256,64,128]{2,1,0:T(8,128)(2,1)S(1)} %get-tuple-element.10.refs_3_), custom_call_target="tpu_custom_call" | custom-call | tf_op jit(solution)/shard_map/score_blocks/pallas_call | solution.py:391
  38.1 18.4 %swap_scores.1 = f32[128,4,128]{2,1,0:T(4,128)S(1)} custom-call(f32[2,256,128]{2,1,0:T(8,128)S(1)} %score_blocks.1.part_ref, s32[10,8,128]{2,1,0:T(8,128)S(1)} %get-tuple-element.8.refs_1_.meta_ref), custom_call_target="tpu_custom_call" | custom-call | tf_op jit(solution)/shard_map/swap_scores/pallas_call | solution.py:449
  56.5 0.7 %copy.6 = f32[128,4,128]{2,1,0:T(4,128)} copy(f32[128,4,128]{2,1,0:T(4,128)S(1)} %swap_scores.1) | data formatting | bytes 524288
Async XLA Ops:
  0.0 28.3 %copy-start = (s32[8,128]{1,0:T(8,128)S(1)}, s32[8,128]{1,0:T(8,128)}, u32[]{:S(2)}) copy-start(s32[8,128]{1,0:T(8,128)} %refs_0_.1) | copy-start | bytes 12292

commit v5 on v4

--- a/solution.py
+++ b/solution.py
@@ -17,6 +17,51 @@
     return {"docs": ((y * 4 + zl) * 4 + x) * 2 + c, "pb": h}
 
 
+def around(idx):
+    c, x, zl, y = idx % 2, (idx // 2) % 4, (idx // 8) % 4, idx // 32
+
+    def at(y, x, c):
+        return ((y * 4 + zl) * 4 + x) * 2 + c
+
+    xp, xm, yp, ym = (x + 1) % 4, (x + 3) % 4, (y + 1) % 4, (y + 3) % 4
+    return c, [[at(v, u, w) for w in (c, 1 - c)] for v, u in ((y, xm), (y, xp), (ym, x), (yp, x))]
+
+
+def sides_of(idx):
+    c, near = around(idx)
+    sides = [(idx, 0, 8, 0, 0), (idx + 1 - 2 * c, 8, 8, 1, 0)]
+    for n in range(4):
+        for o in range(2):
+            sides.append((near[n][o], 16 + 4 * n + 2 * o, 2, 2 + 2 * n + o, 8 + 2 * n))
+    return sides
+
+
+def list_steps(idx, tables, pattern, plan):
+    row = lax.broadcasted_iota(jnp.int32, (32, 128), 0)
+    lane = lax.broadcasted_iota(jnp.int32, (32, 128), 1)
+    col = jnp.zeros((32, 128), jnp.int32)
+    first = jnp.zeros((32, 128), jnp.int32)
+    values = jnp.zeros((32, 128), jnp.int32)
+    for block, here, groups, table, there in sides_of(idx):
+        mine = (row >= here) & (row < here + groups)
+        col = jnp.where(mine, block, col)
+        first = jnp.where(mine, (there + row - here) * 8, first)
+        values = jnp.where(mine, jnp.broadcast_to(tables[table, 3:4], (32, 128)), values)
+    need = jnp.sum(jnp.where(lane == first, values, 0), axis=1, keepdims=True)
+    t = lax.broadcasted_iota(jnp.int32, (32, 384), 1)
+    for k in range(8):
+        flags = jnp.broadcast_to(pattern[k:k + 1], (32, 128))
+        on = jnp.sum(jnp.where(lane == col, flags, 0), axis=1, keepdims=True)
+        size = jnp.where(on > 0, need, 0)
+        turned = jnp.sum(jnp.where(lane == row, size, 0), axis=0, keepdims=True)
+        ends = jnp.sum(jnp.where(lane <= row, turned, 0), axis=1, keepdims=True)
+        steps = jnp.sum(turned, axis=1, keepdims=True)
+        place = jnp.minimum(t, steps - 1)
+        listed = place[0:1] + jnp.sum(jnp.where(ends <= place, 8 - size, 0), axis=0, keepdims=True)
+        plan[k:k + 1, 0:384] = listed
+        plan[k:k + 1, 384:512] = jnp.broadcast_to(steps, (1, 128))
+
+
 SHARES = (0, 2, 4, 6, 9, 11, 13, 15, 1, 14, 3, 12, 5, 10, 7, 8)
 
 
@@ -28,10 +73,10 @@
     return slot * 8 + rank % 8
 
 
-def gather_kernel(q_hbm, len_hbm, d_hbm, q_out, dt_out, meta_out,
-                  q_ref, len_ref, tmp, prep, docs, wide, dt, meta, meta_s, zs, zr, ss, sr, ts, tr, ls):
+def gather_kernel(q_hbm, len_hbm, d_hbm, pat_hbm, q_out, dt_out, meta_out, plan_out,
+                  q_ref, len_ref, pat_ref, tables, plan, tmp, prep, docs, wide, dt, meta, meta_s, zs, zr, ss, sr, ts, tr, ls):
     loads = [pltpu.make_async_copy(src, dst, ls.at[5 + n])
-             for n, (src, dst) in enumerate(((q_hbm, q_ref), (len_hbm, len_ref), (d_hbm, docs)))]
+             for n, (src, dst) in enumerate(((q_hbm, q_ref), (len_hbm, len_ref), (d_hbm, docs), (pat_hbm, pat_ref)))]
     for cp in loads:
         cp.start()
     idx = lax.axis_index("docs")
@@ -186,19 +231,29 @@
         share[4 + n].wait_recv()
         share.append(send(dt_out.at[pl.ds(128 + 32 * n, 16)], dt_out.at[pl.ds(144 + 32 * n, 16)],
                           ts.at[10 + n], tr.at[10 + n], twin))
-    last = share[8:]
+    last = share[12:]
     for xs, ys, pa, pb in ((x, y, a0, b0), (xm, ym, a1, b1), (xp, yp, a2, b2), (x2, y2, a3, b3)):
         last.extend(relay_a(xs, pa))
         last.extend(relay_b(ys, pb))
-    for cp in [m0, m1] + last:
+    for cp in [m0] + share[8:12]:
         cp.wait_recv()
-    for cp in (lo, ld):
+    lt = pltpu.make_async_copy(meta_out, tables, ls.at[9])
+    lo.wait()
+    lt.start()
+    loads[3].wait()
+    lt.wait()
+    list_steps(idx, tables, pat_ref, plan)
+    lp = pltpu.make_async_copy(plan, plan_out, ls.at[10])
+    lp.start()
+    for cp in [m1] + last:
+        cp.wait_recv()
+    for cp in (ld, lp):
         cp.wait()
     for cp in waits:
         cp.wait_send()
 
 
-def gather(queries, lengths, documents):
+def gather(queries, lengths, documents, pattern):
     hbm = pl.BlockSpec(memory_space=pltpu.HBM)
     free = pl.BlockSpec(memory_space=pl.ANY)
     return pl.pallas_call(
@@ -208,12 +263,16 @@
             jax.ShapeDtypeStruct((4, 4, 4, 2, 64, 128), jnp.bfloat16),
             jax.ShapeDtypeStruct((256, CH, 128), jnp.bfloat16),
             jax.ShapeDtypeStruct((10, 8, 128), jnp.int32),
+            jax.ShapeDtypeStruct((8, 512), jnp.int32),
         ),
-        in_specs=[hbm, hbm, hbm],
-        out_specs=(free, free, free),
+        in_specs=[hbm, hbm, hbm, hbm],
+        out_specs=(free, free, free, free),
         scratch_shapes=[
             pltpu.VMEM((8, 16, 128), jnp.bfloat16),
             pltpu.VMEM((1, 128), jnp.int32),
+            pltpu.VMEM((8, 128), jnp.int32),
+            pltpu.VMEM((10, 8, 128), jnp.int32),
+            pltpu.VMEM((8, 512), jnp.int32),
             pltpu.VMEM((64, 128), jnp.float32),
             pltpu.VMEM((2, 64, 128), jnp.bfloat16),
             pltpu.VMEM((128, 64, 128), jnp.bfloat16),
@@ -227,10 +286,10 @@
             pltpu.SemaphoreType.DMA((40,)),
             pltpu.SemaphoreType.DMA((18,)),
             pltpu.SemaphoreType.DMA((18,)),
-            pltpu.SemaphoreType.DMA((8,)),
+            pltpu.SemaphoreType.DMA((11,)),
         ],
         compiler_params=pltpu.CompilerParams(collective_id=0, has_side_effects=True, vmem_limit_bytes=12 << 20),
-    )(*[pltpu.with_memory_space_constraint(v, pltpu.HBM) for v in (queries, lengths, documents)])
+    )(*[pltpu.with_memory_space_constraint(v, pltpu.HBM) for v in (queries, lengths, documents, pattern)])
 
 
 def score_kernel(position, *refs):
@@ -240,52 +299,22 @@
     )
 
 
-def around(idx):
-    c, x, zl, y = idx % 2, (idx // 2) % 4, (idx // 8) % 4, idx // 32
-
-    def at(y, x, c):
-        return ((y * 4 + zl) * 4 + x) * 2 + c
-
-    xp, xm, yp, ym = (x + 1) % 4, (x + 3) % 4, (y + 1) % 4, (y + 3) % 4
-    return c, [[at(v, u, w) for w in (c, 1 - c)] for v, u in ((y, xm), (y, xp), (ym, x), (yp, x))]
-
-
-def score_body(position, pat_ref, meta_vmem, rows, dt, out_ref, amax, total, stage, lists, steps, blocks, needs, sem, *accs):
+def score_body(position, pat_ref, plan, rows, dt, out_ref, amax, total, stage, steps, blocks, *accs):
     acc = (accs[:NS], accs[NS:])
-    copy = pltpu.make_async_copy(meta_vmem.at[:, pl.ds(3, 1)], needs, sem)
-    copy.start()
-    stage[...] = jnp.zeros_like(stage)
-    idx = position()
-    c, near = around(idx)
-    sides = [(idx, 0, 8, 0, 0), (idx + 1 - 2 * c, 8, 8, 1, 0)]
-    for n in range(4):
-        for o in range(2):
-            sides.append((near[n][o], 16 + 4 * n + 2 * o, 2, 2 + 2 * n + o, 8 + 2 * n))
-
-    def listing(k, n):
-        t = jnp.int32(0)
-        for col, here, groups, table, there in sides:
-            def add(t, here=here, groups=groups, table=table, there=there):
-                for g in range(groups):
-                    for i in range(8):
-                        lists[n, t + i] = (here + g) * 8 + i
-                    t = t + needs[table, 0, (there + g) * 8]
-                return t
-
-            t = lax.cond(pat_ref[k, col] > 0, add, lambda t: t, t)
+    sides = sides_of(position())
+
+    def active(k, n):
+        t = plan[k, 384]
 
         @pl.when(t > 0)
         def _():
-            end = lists[n, t - 1]
-            for i in range(RUN):
-                lists[n, t + i] = end
+            blocks[n] = k
             steps[n] = (t + RUN - 1) // RUN
-            blocks[n] = k
 
         return n + (t > 0).astype(jnp.int32)
 
-    copy.wait()
-    count = lax.fori_loop(0, 8, listing, jnp.int32(0))
+    count = lax.fori_loop(0, 8, active, jnp.int32(0))
+    stage[...] = jnp.zeros_like(stage)
 
     def weights(p):
         k = blocks[p]
@@ -331,8 +360,9 @@
         def one_block(p, state):
             p0, last0, tops = state
             n = steps[p]
-            olds = [lists[jnp.maximum(p0, 0), last0 * RUN + s] for s in range(RUN)]
-            news = [lists[p, s] for s in range(RUN)]
+            k, k0 = blocks[p], blocks[jnp.maximum(p0, 0)]
+            olds = [plan[k0, last0 * RUN + s] for s in range(RUN)]
+            news = [plan[k, s] for s in range(RUN)]
             for s in range(RUN):
                 tops = pop(olds[s], s, tops)
                 push(news[s], s, head=s == 0)
@@ -340,8 +370,8 @@
             close(jnp.where(p0 < 0, 8, p0))
 
             def further(m, tops):
-                olds = [lists[p, (m - 1) * RUN + s] for s in range(RUN)]
-                news = [lists[p, m * RUN + s] for s in range(RUN)]
+                olds = [plan[k, (m - 1) * RUN + s] for s in range(RUN)]
+                news = [plan[k, m * RUN + s] for s in range(RUN)]
                 for s in range(RUN):
                     tops = pop(olds[s], s, tops)
                     push(news[s], s)
@@ -353,7 +383,7 @@
         start = [jnp.full((8, 256), -jnp.inf, jnp.float32)] * 4
         p, last, tops = lax.fori_loop(0, count, one_block, (zero - 1, zero, start))
         for s in range(RUN):
-            tops = pop(lists[p, last * RUN + s], s, tops)
+            tops = pop(plan[blocks[p], last * RUN + s], s, tops)
         close(p)
         push(0, 0, head=True)
         for half in range(2):
@@ -385,27 +415,24 @@
             out_ref[side, part * 128:(part + 1) * 128] = stage[side, :, part * 128:(part + 1) * 128].T
 
 
-def score(position, pattern, meta, rows, dt):
+def score(position, pattern, plan, rows, dt):
     smem = pl.BlockSpec(memory_space=pltpu.SMEM)
     vmem = pl.BlockSpec(memory_space=pltpu.VMEM)
     return pl.pallas_call(
         functools.partial(score_kernel, position),
         name="score_blocks",
         out_shape=jax.ShapeDtypeStruct((2, 256, 128), jnp.float32),
-        in_specs=[smem, vmem, vmem, vmem],
+        in_specs=[smem, smem, vmem, vmem],
         out_specs=vmem,
         scratch_shapes=[
             pltpu.VMEM((32, 4, 8, 256), jnp.float32),
             pltpu.VMEM((9, 32, 8, 128), jnp.float32),
             pltpu.VMEM((2, 128, 256), jnp.float32),
-            pltpu.SMEM((8, 256 + NS), jnp.int32),
             pltpu.SMEM((8,), jnp.int32),
             pltpu.SMEM((8,), jnp.int32),
-            pltpu.SMEM((10, 1, 128), jnp.int32),
-            pltpu.SemaphoreType.DMA,
         ],
         compiler_params=pltpu.CompilerParams(vmem_limit_bytes=24 << 20),
-    )(pattern, meta, rows, dt)
+    )(pattern, plan, rows, dt)
 
 
 def swap_kernel(part_ref, meta_ref, out_ref, got, s_sem, r_sem):
@@ -462,8 +489,8 @@
 
 
 def local(queries, documents, lengths, pattern):
-    rows, dt, meta = gather(queries, lengths.reshape(1, 128), documents)
-    part = score(lambda: lax.axis_index("docs"), pattern, meta, rows.reshape(8, 8, 128, 128), dt)
+    rows, dt, meta, plan = gather(queries, lengths.reshape(1, 128), documents, pattern)
+    part = score(lambda: lax.axis_index("docs"), pattern, plan, rows.reshape(8, 8, 128, 128), dt)
     return swap(part, meta)
 
 

time: 57.3 us -> 52.9 us (0.923)
  the two profiles are of different devices: /device:TPU:33 before, /device:TPU:1 now
where the time goes in v5:
time: 52.9 us; the launch traced here: 52.8 us
  Pallas kernels  52 us (98%)
  local copies, waits for them, and re-layouts  0.71 us (1%)
    pallas_call x1, Pallas kernels, gather(): pl.pallas_call(gather_kernel, name='gather_queries', out_shape=(jax.Shape...  30.1 us
    pallas_call x1, Pallas kernels, swap(): pl.pallas_call(swap_kernel, name='swap_scores', out_shape=jax.ShapeDtypeS...  19.3 us
    pallas_call x1, Pallas kernels, score(): pl.pallas_call(functools.partial(score_kernel, position), name='score_blo...  2.6 us

profile of v5, /device:TPU:1, one launch (start us, length us, event | category | flops | bytes accessed | tf_op | source)
XLA Modules:
  0.0 52.8 jit_solution(4651219328650797648)
XLA Ops:
  0.0 0.0 copy-start
  0.0 30.1 %gather_queries.1 = (bf16[4,4,4,2,64,128]{5,4,3,2,1,0:T(8,128)(2,1)S(1)}, bf16[256,64,128]{2,1,0:T(8,128)(2,1)S(1)}, s32[10,8,128]{2,1,0:T(8,128)S(1)}, s32[8,512]{1,0:T(8,128)S(1)}) custom-call(bf16[8,16,128]{2,1,0:T(8,128)(2,1)} %q_hbm.1, s32[1,128]{1,0:T(1,128)} %bitcast.3, bf16[128,64,128]{2,1,0:T(8,128)(2,1)} %d_hbm.1, s32[8,128]{1,0:T(8,128)} %refs_0_.1), custom_call_target="tpu_custom_call" | custom-call | tf_op jit(solution)/shard_map/gather_queries/pallas_call | solution.py:259
  30.1 0.0 copy-done
  30.1 2.6 %score_blocks.1.part_ref = f32[2,256,128]{2,1,0:T(8,128)S(1)} custom-call(s32[8,128]{1,0:T(8,128)S(1)} %copy-done, s32[8,512]{1,0:T(8,128)S(1)} %get-tuple-element.9.refs_1_, bf16[8,8,128,128]{3,2,1,0:T(8,128)(2,1)S(1)} %bitcast.2, bf16[256,64,128]{2,1,0:T(8,128)(2,1)S(1)} %get-tuple-element.11.refs_3_), custom_call_target="tpu_custom_call" | custom-call | tf_op jit(solution)/shard_map/score_blocks/pallas_call | solution.py:421
  32.7 19.3 %swap_scores.1 = f32[128,4,128]{2,1,0:T(4,128)S(1)} custom-call(f32[2,256,128]{2,1,0:T(8,128)S(1)} %score_blocks.1.part_ref, s32[10,8,128]{2,1,0:T(8,128)S(1)} %get-tuple-element.12.meta_ref), custom_call_target="tpu_custom_call" | custom-call | tf_op jit(solution)/shard_map/swap_scores/pallas_call | solution.py:476
  52.1 0.7 %copy.6 = f32[128,4,128]{2,1,0:T(4,128)} copy(f32[128,4,128]{2,1,0:T(4,128)S(1)} %swap_scores.1) | data formatting | bytes 524288
Async XLA Ops:
  0.0 30.1 %copy-start = (s32[8,128]{1,0:T(8,128)S(1)}, s32[8,128]{1,0:T(8,128)}, u32[]{:S(2)}) copy-start(s32[8,128]{1,0:T(8,128)} %refs_0_.1) | copy-start | bytes 12292

commit v6 on v5

--- a/solution.py
+++ b/solution.py
@@ -221,20 +221,22 @@
     a2 = spread_a(xp)
     b1 = spread_b(ym)
     b2 = spread_b(yp)
+    early = list(relay_a(x, a0)) + list(relay_b(y, b0))
     s4.wait_recv()
     s5.wait_recv()
     a3 = spread_a(x2)
     s6.wait_recv()
     s7.wait_recv()
     b3 = spread_b(y2)
-    for n in range(4):
-        share[4 + n].wait_recv()
-        share.append(send(dt_out.at[pl.ds(128 + 32 * n, 16)], dt_out.at[pl.ds(144 + 32 * n, 16)],
-                          ts.at[10 + n], tr.at[10 + n], twin))
-    last = share[12:]
-    for xs, ys, pa, pb in ((x, y, a0, b0), (xm, ym, a1, b1), (xp, yp, a2, b2), (x2, y2, a3, b3)):
+    last = early
+    for xs, ys, pa, pb in ((xm, ym, a1, b1), (xp, yp, a2, b2), (x2, y2, a3, b3)):
         last.extend(relay_a(xs, pa))
         last.extend(relay_b(ys, pb))
+        if xs is xm:
+            for n in range(4):
+                share[4 + n].wait_recv()
+                share.append(send(dt_out.at[pl.ds(128 + 32 * n, 16)], dt_out.at[pl.ds(144 + 32 * n, 16)],
+                                  ts.at[10 + n], tr.at[10 + n], twin))
     for cp in [m0] + share[8:12]:
         cp.wait_recv()
     lt = pltpu.make_async_copy(meta_out, tables, ls.at[9])
@@ -245,7 +247,7 @@
     list_steps(idx, tables, pat_ref, plan)
     lp = pltpu.make_async_copy(plan, plan_out, ls.at[10])
     lp.start()
-    for cp in [m1] + last:
+    for cp in [m1] + share[12:] + last:
         cp.wait_recv()
     for cp in (ld, lp):
         cp.wait()
@@ -459,9 +461,9 @@
         cp.start()
     got[c, :, 0:64] = part_ref[:, 0:64]
     rank = jnp.broadcast_to(meta_ref[0, 1:2], (128, 128))
-    for cp in copies:
-        cp.wait_recv()
-    for core in range(2):
+    for core, arrivals in ((c, copies[0:8:2]), (1 - c, copies[1:8:2] + copies[8:])):
+        for cp in arrivals:
+            cp.wait_recv()
         for half in range(2):
             back = jnp.take_along_axis(got[core, half].T, rank, axis=1).reshape(4, 8, 4, 128)
             for k in range(4):

time: 52.9 us -> 50.6 us (0.957)
  the two profiles are of different devices: /device:TPU:1 before, /device:TPU:66 now
where the time goes in v6:
time: 50.6 us; the launch traced here: 50.7 us
  Pallas kernels  50 us (99%)
  local copies, waits for them, and re-layouts  0.71 us (1%)
    pallas_call x1, Pallas kernels, gather(): pl.pallas_call(gather_kernel, name='gather_queries', out_shape=(jax.Shape...  29.3 us
    pallas_call x1, Pallas kernels, swap(): pl.pallas_call(swap_kernel, name='swap_scores', out_shape=jax.ShapeDtypeS...  13.4 us
    pallas_call x1, Pallas kernels, score(): pl.pallas_call(functools.partial(score_kernel, position), name='score_blo...  7.31 us

profile of v6, /device:TPU:66, one launch (start us, length us, event | category | flops | bytes accessed | tf_op | source)
XLA Modules:
  0.0 50.7 jit_solution(6301023768394141387)
XLA Ops:
  0.0 0.0 copy-start
  0.0 29.3 %gather_queries.1 = (bf16[4,4,4,2,64,128]{5,4,3,2,1,0:T(8,128)(2,1)S(1)}, bf16[256,64,128]{2,1,0:T(8,128)(2,1)S(1)}, s32[10,8,128]{2,1,0:T(8,128)S(1)}, s32[8,512]{1,0:T(8,128)S(1)}) custom-call(bf16[8,16,128]{2,1,0:T(8,128)(2,1)} %q_hbm.1, s32[1,128]{1,0:T(1,128)} %bitcast.3, bf16[128,64,128]{2,1,0:T(8,128)(2,1)} %d_hbm.1, s32[8,128]{1,0:T(8,128)} %refs_0_.1), custom_call_target="tpu_custom_call" | custom-call | tf_op jit(solution)/shard_map/gather_queries/pallas_call | solution.py:261
  29.3 0.0 copy-done
  29.3 7.3 %score_blocks.1.part_ref = f32[2,256,128]{2,1,0:T(8,128)S(1)} custom-call(s32[8,128]{1,0:T(8,128)S(1)} %copy-done, s32[8,512]{1,0:T(8,128)S(1)} %get-tuple-element.9.refs_1_, bf16[8,8,128,128]{3,2,1,0:T(8,128)(2,1)S(1)} %bitcast.2, bf16[256,64,128]{2,1,0:T(8,128)(2,1)S(1)} %get-tuple-element.11.refs_3_), custom_call_target="tpu_custom_call" | custom-call | tf_op jit(solution)/shard_map/score_blocks/pallas_call | solution.py:423
  36.6 13.4 %swap_scores.1 = f32[128,4,128]{2,1,0:T(4,128)S(1)} custom-call(f32[2,256,128]{2,1,0:T(8,128)S(1)} %score_blocks.1.part_ref, s32[10,8,128]{2,1,0:T(8,128)S(1)} %get-tuple-element.12.meta_ref), custom_call_target="tpu_custom_call" | custom-call | tf_op jit(solution)/shard_map/swap_scores/pallas_call | solution.py:478
  50.0 0.7 %copy.6 = f32[128,4,128]{2,1,0:T(4,128)} copy(f32[128,4,128]{2,1,0:T(4,128)S(1)} %swap_scores.1) | data formatting | bytes 524288
Async XLA Ops:
  0.0 29.3 %copy-start = (s32[8,128]{1,0:T(8,128)S(1)}, s32[8,128]{1,0:T(8,128)}, u32[]{:S(2)}) copy-start(s32[8,128]{1,0:T(8,128)} %refs_0_.1) | copy-start | bytes 12292
